TPU v7x, 512 devices: a whole 4x4x16 slice. The times are simulated.
512 devices in a mesh: tm: 16 (over y, x_lo, core), strip: 32 (over z, x_hi).
Axes of the slice: x: 4 (x_hi: 2, x_lo: 2; x = x_hi * 2 + x_lo), y: 4, z: 16, core: 2. Of those that a mesh axis runs over, the one named last changes fastest.
Arguments:
- increment: float32 [16, 3, 1024, 384], P('tm', None, 'strip'), may hold values from -6 to 6
- ref_depth: float32 [16, 1, 1024, 384], P('tm', None, 'strip'), may hold values from 0.6 to 1.4
- ref_wind: float32 [16, 2, 1024, 384], P('tm', None, 'strip'), may hold values from -0.5 to 0.5
- spread: float32 [16, 3, 1024, 384], P('tm', None, 'strip'), may hold values from 0.5 to 2
- decay: float32 [16, 3, 1024, 384], P('tm', None, 'strip'), may hold values from 0.3 to 0.97
Outputs:
- product: float32 [16, 3, 1024, 384], P('tm', None, 'strip')
All inputs are finite; a program needn't handle non-finite values.
Results may differ from a plain program's by a relative error of at most 0.00011.
Values sent between devices are 32-bit elements; how exact they have to be, the bound alone decides.
A program may use at most 64 MiB of HBM per device.

v0:
```python
import jax
import jax.numpy as jnp
from jax import lax
from jax.sharding import Mesh
from jax.sharding import PartitionSpec as P

STEPS = 12
TM = ("tm_0", "tm_1", "tm_2")


time_step = 0.4
gravity = 1.0


def with_halo(block, sides, width):
    for axis, dim in sides:
        count = lax.axis_size(axis)
        forward = [(i, i + 1) for i in range(count - 1)]
        backward = [(target, source) for source, target in forward]
        low = lax.ppermute(
            lax.slice_in_dim(block, block.shape[dim] - width, None, axis=dim), axis, forward
        )
        high = lax.ppermute(lax.slice_in_dim(block, 0, width, axis=dim), axis, backward)
        block = jnp.concatenate([low, block, high], axis=dim)
    return block


def shifted(value, axis, steps):
    count = lax.axis_size(axis)
    initial, last = (max(0, -steps), min(count, count - steps))
    return lax.ppermute(value, axis, [(source, source + steps) for source in range(initial, last)])


def nothing_yet(x, identity):
    return jax.tree.map(
        lambda a, e: jnp.broadcast_to(jnp.asarray(e, a.dtype), a.shape), x, identity
    )


def prefix_by_axis(x, axes, combine, identity, reverse):
    before = start = nothing_yet(x, identity)
    total = x
    for axis in reversed(axes):
        devices, index = (lax.axis_size(axis), lax.axis_index(axis))
        pieces = jax.tree.map(lambda part: lax.all_gather(part, axis), total)
        inside, total = (start, start)
        for k in reversed(range(devices)) if reverse else range(devices):
            passed = k > index if reverse else k < index
            total = combine(total, jax.tree.map(lambda part: part[k], pieces))
            inside = jax.tree.map(lambda new, old: jnp.where(passed, new, old), total, inside)
        before = combine(inside, before)
    return before


def inner(field):
    return field[..., 1:-1, :]


def along_x(field):
    return (0.5 * (jnp.roll(field, -1, -1) - jnp.roll(field, 1, -1)))[..., 1:-1, :]


def along_y(field):
    return 0.5 * (field[..., 2:, :] - field[..., :-2, :])


def model_step(padded, ref_padded, first_row, total_rows):
    height = padded[..., 0, :, :]
    east_flow = padded[..., 1, :, :]
    north_flow = padded[..., 2, :, :]
    depth_ref = ref_padded[..., 0, :, :]
    east_ref = ref_padded[..., 1, :, :]
    north_ref = ref_padded[..., 2, :, :]
    out_rows = padded.shape[-2] - 2
    row_ids = first_row + jnp.arange(out_rows, dtype=jnp.int32)
    coriolis = (0.2 + 0.4 * row_ids.astype(jnp.float32) / total_rows)[:, None]
    inside = ((row_ids >= 0) & (row_ids < total_rows)).astype(jnp.float32)[:, None]
    flux_east = depth_ref * east_flow + east_ref * height
    flux_north = depth_ref * north_flow + north_ref * height
    new_height = inner(height) - time_step * (along_x(flux_east) + along_y(flux_north))
    new_east = inner(east_flow) - time_step * (
        inner(east_ref) * along_x(east_flow)
        + inner(north_ref) * along_y(east_flow)
        + gravity * along_x(height)
        - coriolis * inner(north_flow)
    )
    new_north = inner(north_flow) - time_step * (
        inner(east_ref) * along_x(north_flow)
        + inner(north_ref) * along_y(north_flow)
        + gravity * along_y(height)
        + coriolis * inner(east_flow)
    )
    return jnp.stack([new_height, new_east, new_north], axis=-3) * inside


def compose(former, latter):
    return (former[0] * latter[0], latter[0] * former[1] + latter[1])


def body(increment, ref_depth, ref_wind, spread, decay):
    rows_dev = increment.shape[2]
    total_rows = rows_dev * lax.axis_size("strip")
    base_row = lax.axis_index("strip") * rows_dev
    references = jnp.concatenate([ref_depth, ref_wind], axis=1)
    ref_deep = with_halo(references, (("strip", 2),), 4)

    def ref_slice(margin):
        return ref_deep[:, :, 4 - margin : 4 + rows_dev + margin]

    def advance(padded):
        for margin in range(4, 0, -1):
            padded = model_step(padded, ref_slice(margin), base_row - margin + 1, total_rows)
        return padded

    fields = increment
    for repeat in range(STEPS // 4):
        fields = advance(with_halo(fields, (("strip", 2),), 4))
    tangent = fields
    zero_padded = jnp.zeros(increment.shape[:2] + (rows_dev + 8, increment.shape[3]), jnp.float32)
    _, pull_block = jax.vjp(advance, zero_padded)
    carried = shifted(tangent, TM, 1)
    residual = increment - carried
    scaled = spread * residual
    ones_field = jnp.ones_like(scaled)
    zero_field = jnp.zeros_like(scaled)
    prefix = prefix_by_axis((decay, scaled), TM, compose, (ones_field, zero_field), False)
    built = decay * prefix[1] + scaled
    suffix = prefix_by_axis((decay, decay * built), TM, compose, (ones_field, zero_field), True)
    smoothed = built + suffix[1]
    weighted = spread * smoothed
    following = shifted(weighted, TM, -1)
    fields = following
    for repeat in range(STEPS // 4):
        pulled = pull_block(fields)[0]
        rim_rows = jnp.concatenate([pulled[:, :, :4], pulled[:, :, -4:]], axis=2)
        outer = with_halo(rim_rows, (("strip", 2),), 4)
        fields = pulled[:, :, 4 : 4 + rows_dev]
        fields = fields.at[:, :, :4].add(outer[:, :, :4])
        fields = fields.at[:, :, -4:].add(outer[:, :, 12:])
    return weighted - fields


def solution(mesh):
    split = Mesh(
        mesh.devices.reshape(4, 2, 2, mesh.shape["strip"]), ("tm_0", "tm_1", "tm_2", "strip")
    )
    return jax.shard_map(
        body,
        mesh=split,
        in_specs=(
            P(TM, None, "strip", None),
            P(TM, None, "strip", None),
            P(TM, None, "strip", None),
            P(TM, None, "strip", None),
            P(TM, None, "strip", None),
        ),
        out_specs=P(TM, None, "strip", None),
        check_vma=False,
    )
```

profile of v0, /device:TPU:162, one launch (start us, length us, event | category | flops | bytes accessed | tf_op | source)
XLA Modules:
  0.0 191.2 jit_solution(14911881531938386768)
XLA Ops:
  0.0 0.8 constant_dynamic-update-slice_fusion.1
  0.9 4.2 %collective-permute-start.2 = (f32[1,3,4,384]{3,2,1,0:T(4,128)S(1)}, f32[1,3,4,384]{3,2,1,0:T(4,128)S(1)}, u32[]{:S(2)}, u32[]{:S(2)}) collective-permute-start(f32[1,3,4,384]{3,2,1,0:T(4,128)S(1)} %get-tuple-element.413), channel_id=1, source_target_pairs={{0,1},{1,2},{2,3},{3,4},{4,5},{5,6},{6,7},{7,8},{8,9},{9,10},{10,1... | collective-permute-start | bytes 55304 | tf_op jit(solution)/shard_map/ppermute | solution.py:20
  5.1 4.2 %collective-permute-start.3 = (f32[1,3,4,384]{3,2,1,0:T(4,128)S(1)}, f32[1,3,4,384]{3,2,1,0:T(4,128)S(1)}, u32[]{:S(2)}, u32[]{:S(2)}) collective-permute-start(f32[1,3,4,384]{3,2,1,0:T(4,128)S(1)} %get-tuple-element.414), channel_id=1, source_target_pairs={{1,0},{2,1},{3,2},{4,3},{5,4},{6,5},{7,6},{8,7},{9,8},{10,9},{11,1... | collective-permute-start | bytes 55304 | tf_op jit(solution)/shard_map/ppermute | solution.py:23
  9.4 3.1 %collective-permute-start = (f32[1,3,4,384]{3,2,1,0:T(4,128)S(1)}, f32[1,3,4,384]{3,2,1,0:T(4,128)S(1)}, u32[]{:S(2)}, u32[]{:S(2)}) collective-permute-start(f32[1,3,4,384]{3,2,1,0:T(4,128)S(1)} %get-tuple-element.415), channel_id=1, source_target_pairs={{0,1},{1,2},{2,3},{3,4},{4,5},{5,6},{6,7},{7,8},{8,9},{9,10},{10,1... | collective-permute-start | bytes 55304 | tf_op jit(solution)/shard_map/ppermute | solution.py:20
  12.5 5.1 %collective-permute-start.1 = (f32[1,3,4,384]{3,2,1,0:T(4,128)S(1)}, f32[1,3,4,384]{3,2,1,0:T(4,128)S(1)}, u32[]{:S(2)}, u32[]{:S(2)}) collective-permute-start(f32[1,3,4,384]{3,2,1,0:T(4,128)S(1)} %get-tuple-element.416), channel_id=1, source_target_pairs={{1,0},{2,1},{3,2},{4,3},{5,4},{6,5},{7,6},{8,7},{9,8},{10,9},{11,1... | collective-permute-start | bytes 55304 | tf_op jit(solution)/shard_map/ppermute | solution.py:23
  17.8 2.0 %collective-permute-done.1 = f32[1,3,4,384]{3,2,1,0:T(4,128)S(1)} collective-permute-done((f32[1,3,4,384]{3,2,1,0:T(4,128)S(1)}, f32[1,3,4,384]{3,2,1,0:T(4,128)S(1)}, u32[]{:S(2)}, u32[]{:S(2)}) %collective-permute-start.1) | collective-permute-done | bytes 18464 | tf_op jit(solution)/shard_map/ppermute | solution.py:23
  20.6 0.1 fusion.304
  21.8 0.1 fusion.272
  23.0 0.1 fusion.240
  24.4 6.3 %collective-permute-start.4 = (f32[1,3,4,384]{3,2,1,0:T(4,128)S(1)}, f32[1,3,4,384]{3,2,1,0:T(4,128)S(1)}, u32[]{:S(2)}, u32[]{:S(2)}) collective-permute-start(f32[1,3,4,384]{3,2,1,0:T(4,128)S(1)} %get-tuple-element.411), channel_id=1, source_target_pairs={{0,1},{1,2},{2,3},{3,4},{4,5},{5,6},{6,7},{7,8},{8,9},{9,10},{10,1... | collective-permute-start | bytes 55304 | tf_op jit(solution)/shard_map/ppermute | solution.py:20
  30.7 1.9 %collective-permute-start.5 = (f32[1,3,4,384]{3,2,1,0:T(4,128)S(1)}, f32[1,3,4,384]{3,2,1,0:T(4,128)S(1)}, u32[]{:S(2)}, u32[]{:S(2)}) collective-permute-start(f32[1,3,4,384]{3,2,1,0:T(4,128)S(1)} %get-tuple-element.412), channel_id=1, source_target_pairs={{1,0},{2,1},{3,2},{4,3},{5,4},{6,5},{7,6},{8,7},{9,8},{10,9},{11,1... | collective-permute-start | bytes 55304 | tf_op jit(solution)/shard_map/ppermute | solution.py:23
  32.6 5.2 %collective-permute-done.5 = f32[1,3,4,384]{3,2,1,0:T(4,128)S(1)} collective-permute-done((f32[1,3,4,384]{3,2,1,0:T(4,128)S(1)}, f32[1,3,4,384]{3,2,1,0:T(4,128)S(1)}, u32[]{:S(2)}, u32[]{:S(2)}) %collective-permute-start.5) | collective-permute-done | bytes 18464 | tf_op jit(solution)/shard_map/ppermute | solution.py:23
  38.8 0.1 fusion.208
  40.0 0.1 fusion.176
  41.1 0.1 fusion.144
  42.5 3.3 %collective-permute-start.6 = (f32[1,3,4,384]{3,2,1,0:T(4,128)S(1)}, f32[1,3,4,384]{3,2,1,0:T(4,128)S(1)}, u32[]{:S(2)}, u32[]{:S(2)}) collective-permute-start(f32[1,3,4,384]{3,2,1,0:T(4,128)S(1)} %get-tuple-element.409), channel_id=1, source_target_pairs={{0,1},{1,2},{2,3},{3,4},{4,5},{5,6},{6,7},{7,8},{8,9},{9,10},{10,1... | collective-permute-start | bytes 55304 | tf_op jit(solution)/shard_map/ppermute | solution.py:20
  45.8 5.0 %collective-permute-start.7 = (f32[1,3,4,384]{3,2,1,0:T(4,128)S(1)}, f32[1,3,4,384]{3,2,1,0:T(4,128)S(1)}, u32[]{:S(2)}, u32[]{:S(2)}) collective-permute-start(f32[1,3,4,384]{3,2,1,0:T(4,128)S(1)} %get-tuple-element.410), channel_id=1, source_target_pairs={{1,0},{2,1},{3,2},{4,3},{5,4},{6,5},{7,6},{8,7},{9,8},{10,9},{11,1... | collective-permute-start | bytes 55304 | tf_op jit(solution)/shard_map/ppermute | solution.py:23
  50.8 2.2 %collective-permute-done.7 = f32[1,3,4,384]{3,2,1,0:T(4,128)S(1)} collective-permute-done((f32[1,3,4,384]{3,2,1,0:T(4,128)S(1)}, f32[1,3,4,384]{3,2,1,0:T(4,128)S(1)}, u32[]{:S(2)}, u32[]{:S(2)}) %collective-permute-start.7) | collective-permute-done | bytes 18464 | tf_op jit(solution)/shard_map/ppermute | solution.py:23
  53.9 0.1 fusion.112
  55.0 0.1 fusion.80
  56.2 0.1 fusion.48
  57.6 2.1 %collective-permute-start.8 = (f32[1,3,32,384]{3,2,1,0:T(8,128)S(1)}, f32[1,3,32,384]{3,2,1,0:T(8,128)S(1)}, u32[]{:S(2)}, u32[]{:S(2)}) collective-permute-start(f32[1,3,32,384]{3,2,1,0:T(8,128)S(1)} %maximum_multiply_fusion.11), channel_id=1, source_target_pairs={{0,32},{32,64},{64,96},{96,128},{128,160},{160,192},{192,224},{224... | collective-permute-start | bytes 442376 | tf_op jit(solution)/shard_map/ppermute | solution.py:31
  59.6 4.1 %all-gather = f32[2,3,32,384]{3,2,1,0:T(8,128)S(1)} all-gather(f32[1,3,32,384]{3,2,1,0:T(8,128)S(1)} %copy-done.1), channel_id=2, replica_groups=mesh['tm_0'=4,'tm_1'=2,'tm_2'=2,'strip'=32] {'tm_2'}, dimensions={0}, use_global_device_ids=true | all-gather | bytes 442368 | tf_op jit(solution)/shard_map/all_gather | solution.py:45
  63.7 0.5 collective-permute-done.8
  64.2 2.0 %all-gather.1 = f32[2,3,32,384]{3,2,1,0:T(8,128)S(1)} all-gather(f32[1,3,32,384]{3,2,1,0:T(8,128)S(1)} %subtract_multiply_fusion), channel_id=3, replica_groups=mesh['tm_0'=4,'tm_1'=2,'tm_2'=2,'strip'=32] {'tm_2'}, dimensions={0}, use_global_device_ids=true | all-gather | bytes 442368 | tf_op jit(solution)/shard_map/all_gather | solution.py:45
  66.3 6.6 %all_gather.50 = f32[2,1,3,32,384]{4,3,2,1,0:T(8,128)S(1)} all-gather(f32[1,1,3,32,384]{4,3,2,1,0:T(8,128)S(1)} %get-tuple-element.153), channel_id=1, replica_groups=mesh['tm_0'=4,'tm_1'=2,'tm_2'=2,'strip'=32] {'tm_1'}, dimensions={0}, use_global_device_ids=true | all-gather | bytes 442368 | tf_op jit(solution)/shard_map/all_gather | solution.py:45
  72.8 5.8 %all_gather.54 = f32[2,1,3,32,384]{4,3,2,1,0:T(8,128)S(1)} all-gather(f32[1,1,3,32,384]{4,3,2,1,0:T(8,128)S(1)} %get-tuple-element.154), channel_id=1, replica_groups=mesh['tm_0'=4,'tm_1'=2,'tm_2'=2,'strip'=32] {'tm_1'}, dimensions={0}, use_global_device_ids=true | all-gather | bytes 442368 | tf_op jit(solution)/shard_map/all_gather | solution.py:45
  78.7 14.6 %all_gather.51 = f32[4,1,3,32,384]{4,3,2,1,0:T(8,128)S(1)} all-gather(f32[1,1,3,32,384]{4,3,2,1,0:T(8,128)S(1)} %get-tuple-element.151), channel_id=1, replica_groups=mesh['tm_0'=4,'tm_1'=2,'tm_2'=2,'strip'=32] {'tm_0'}, dimensions={0}, use_global_device_ids=true | all-gather | bytes 737280 | tf_op jit(solution)/shard_map/all_gather | solution.py:45
  93.3 13.4 %all_gather.55 = f32[4,1,3,32,384]{4,3,2,1,0:T(8,128)S(1)} all-gather(f32[1,1,3,32,384]{4,3,2,1,0:T(8,128)S(1)} %get-tuple-element.152), channel_id=1, replica_groups=mesh['tm_0'=4,'tm_1'=2,'tm_2'=2,'strip'=32] {'tm_0'}, dimensions={0}, use_global_device_ids=true | all-gather | bytes 737280 | tf_op jit(solution)/shard_map/all_gather | solution.py:45
  106.7 0.3 fusion.516
  106.9 2.0 %all-gather.2 = f32[2,3,32,384]{3,2,1,0:T(8,128)S(1)} all-gather(f32[1,3,32,384]{3,2,1,0:T(8,128)S(1)} %get-tuple-element.125), channel_id=4, replica_groups=mesh['tm_0'=4,'tm_1'=2,'tm_2'=2,'strip'=32] {'tm_2'}, dimensions={0}, use_global_device_ids=true | all-gather | bytes 442368 | tf_op jit(solution)/shard_map/all_gather | solution.py:45
  109.0 6.6 %all_gather.58 = f32[2,1,3,32,384]{4,3,2,1,0:T(8,128)S(1)} all-gather(f32[1,1,3,32,384]{4,3,2,1,0:T(8,128)S(1)} %bitcast_add_fusion.2), channel_id=1, replica_groups=mesh['tm_0'=4,'tm_1'=2,'tm_2'=2,'strip'=32] {'tm_1'}, dimensions={0}, use_global_device_ids=true | all-gather | bytes 442368 | tf_op jit(solution)/shard_map/all_gather | solution.py:45
  115.6 13.3 %all_gather.59 = f32[4,1,3,32,384]{4,3,2,1,0:T(8,128)S(1)} all-gather(f32[1,1,3,32,384]{4,3,2,1,0:T(8,128)S(1)} %multiply_add_fusion), channel_id=1, replica_groups=mesh['tm_0'=4,'tm_1'=2,'tm_2'=2,'strip'=32] {'tm_0'}, dimensions={0}, use_global_device_ids=true | all-gather | bytes 737280 | tf_op jit(solution)/shard_map/all_gather | solution.py:45
  128.9 0.3 fusion.5
  129.2 1.9 %collective-permute-start.9 = (f32[1,3,32,384]{3,2,1,0:T(8,128)S(1)}, f32[1,3,32,384]{3,2,1,0:T(8,128)S(1)}, u32[]{:S(2)}, u32[]{:S(2)}) collective-permute-start(f32[1,3,32,384]{3,2,1,0:T(8,128)S(1)} %fusion.5), channel_id=1, source_target_pairs={{32,0},{64,32},{96,64},{128,96},{160,128},{192,160},{224,192},{256... | collective-permute-start | bytes 442376 | tf_op jit(solution)/shard_map/ppermute | solution.py:31
  131.1 2.6 %collective-permute-done.9 = f32[1,3,32,384]{3,2,1,0:T(8,128)S(1)} collective-permute-done((f32[1,3,32,384]{3,2,1,0:T(8,128)S(1)}, f32[1,3,32,384]{3,2,1,0:T(8,128)S(1)}, u32[]{:S(2)}, u32[]{:S(2)}) %collective-permute-start.9) | collective-permute-done | bytes 147488 | tf_op jit(solution)/shard_map/ppermute | solution.py:31
  134.8 0.1 add_bitcast_fusion.33
  136.1 0.1 add_bitcast_fusion.30
  136.2 0.1 add_bitcast_fusion.31
  137.4 0.1 add_bitcast_fusion.27
  137.6 0.1 add_bitcast_fusion.28
  138.7 0.1 add_bitcast_fusion.24
  139.0 6.7 %collective-permute-start.10 = (f32[1,3,4,384]{3,2,1,0:T(4,128)S(1)}, f32[1,3,4,384]{3,2,1,0:T(4,128)S(1)}, u32[]{:S(2)}, u32[]{:S(2)}) collective-permute-start(f32[1,3,4,384]{3,2,1,0:T(4,128)S(1)} %get-tuple-element.286), channel_id=1, source_target_pairs={{0,1},{1,2},{2,3},{3,4},{4,5},{5,6},{6,7},{7,8},{8,9},{9,10},{10,1... | collective-permute-start | bytes 55304 | tf_op jit(solution)/shard_map/ppermute | solution.py:20
  145.8 2.1 %collective-permute-start.11 = (f32[1,3,4,384]{3,2,1,0:T(4,128)S(1)}, f32[1,3,4,384]{3,2,1,0:T(4,128)S(1)}, u32[]{:S(2)}, u32[]{:S(2)}) collective-permute-start(f32[1,3,4,384]{3,2,1,0:T(4,128)S(1)} %get-tuple-element.285), channel_id=1, source_target_pairs={{1,0},{2,1},{3,2},{4,3},{5,4},{6,5},{7,6},{8,7},{9,8},{10,9},{11,1... | collective-permute-start | bytes 55304 | tf_op jit(solution)/shard_map/ppermute | solution.py:23
  147.9 5.0 %collective-permute-done.11 = f32[1,3,4,384]{3,2,1,0:T(4,128)S(1)} collective-permute-done((f32[1,3,4,384]{3,2,1,0:T(4,128)S(1)}, f32[1,3,4,384]{3,2,1,0:T(4,128)S(1)}, u32[]{:S(2)}, u32[]{:S(2)}) %collective-permute-start.11) | collective-permute-done | bytes 18464 | tf_op jit(solution)/shard_map/ppermute | solution.py:23
  154.0 0.1 add_bitcast_fusion.21
  155.3 0.1 add_bitcast_fusion.18
  155.4 0.1 add_bitcast_fusion.19
  156.6 0.1 add_bitcast_fusion.15
  156.7 0.1 add_bitcast_fusion.16
  157.9 0.1 add_bitcast_fusion.12
  158.2 6.3 %collective-permute-start.12 = (f32[1,3,4,384]{3,2,1,0:T(4,128)S(1)}, f32[1,3,4,384]{3,2,1,0:T(4,128)S(1)}, u32[]{:S(2)}, u32[]{:S(2)}) collective-permute-start(f32[1,3,4,384]{3,2,1,0:T(4,128)S(1)} %get-tuple-element.245), channel_id=1, source_target_pairs={{0,1},{1,2},{2,3},{3,4},{4,5},{5,6},{6,7},{7,8},{8,9},{9,10},{10,1... | collective-permute-start | bytes 55304 | tf_op jit(solution)/shard_map/ppermute | solution.py:20
  164.6 1.9 %collective-permute-start.13 = (f32[1,3,4,384]{3,2,1,0:T(4,128)S(1)}, f32[1,3,4,384]{3,2,1,0:T(4,128)S(1)}, u32[]{:S(2)}, u32[]{:S(2)}) collective-permute-start(f32[1,3,4,384]{3,2,1,0:T(4,128)S(1)} %get-tuple-element.244), channel_id=1, source_target_pairs={{1,0},{2,1},{3,2},{4,3},{5,4},{6,5},{7,6},{8,7},{9,8},{10,9},{11,1... | collective-permute-start | bytes 55304 | tf_op jit(solution)/shard_map/ppermute | solution.py:23
  166.5 5.2 %collective-permute-done.13 = f32[1,3,4,384]{3,2,1,0:T(4,128)S(1)} collective-permute-done((f32[1,3,4,384]{3,2,1,0:T(4,128)S(1)}, f32[1,3,4,384]{3,2,1,0:T(4,128)S(1)}, u32[]{:S(2)}, u32[]{:S(2)}) %collective-permute-start.13) | collective-permute-done | bytes 18464 | tf_op jit(solution)/shard_map/ppermute | solution.py:23
  172.8 0.1 add_bitcast_fusion.9
  174.1 0.1 add_bitcast_fusion.6
  174.2 0.1 add_bitcast_fusion.7
  175.4 0.1 add_bitcast_fusion.3
  175.5 0.1 add_bitcast_fusion.4
  176.7 0.1 add_bitcast_fusion
  177.0 6.3 %collective-permute-start.14 = (f32[1,3,4,384]{3,2,1,0:T(4,128)S(1)}, f32[1,3,4,384]{3,2,1,0:T(4,128)S(1)}, u32[]{:S(2)}, u32[]{:S(2)}) collective-permute-start(f32[1,3,4,384]{3,2,1,0:T(4,128)S(1)} %get-tuple-element.204), channel_id=1, source_target_pairs={{0,1},{1,2},{2,3},{3,4},{4,5},{5,6},{6,7},{7,8},{8,9},{9,10},{10,1... | collective-permute-start | bytes 55304 | tf_op jit(solution)/shard_map/ppermute | solution.py:20
  183.3 1.9 %collective-permute-start.15 = (f32[1,3,4,384]{3,2,1,0:T(4,128)S(1)}, f32[1,3,4,384]{3,2,1,0:T(4,128)S(1)}, u32[]{:S(2)}, u32[]{:S(2)}) collective-permute-start(f32[1,3,4,384]{3,2,1,0:T(4,128)S(1)} %get-tuple-element.203), channel_id=1, source_target_pairs={{1,0},{2,1},{3,2},{4,3},{5,4},{6,5},{7,6},{8,7},{9,8},{10,9},{11,1... | collective-permute-start | bytes 55304 | tf_op jit(solution)/shard_map/ppermute | solution.py:23
  185.3 5.2 %collective-permute-done.15 = f32[1,3,4,384]{3,2,1,0:T(4,128)S(1)} collective-permute-done((f32[1,3,4,384]{3,2,1,0:T(4,128)S(1)}, f32[1,3,4,384]{3,2,1,0:T(4,128)S(1)}, u32[]{:S(2)}, u32[]{:S(2)}) %collective-permute-start.15) | collective-permute-done | bytes 18464 | tf_op jit(solution)/shard_map/ppermute | solution.py:23
  190.5 0.7 sub.983
  (464 shorter events, 25.1 us)
Async XLA Ops:
  0.0 0.9 copy-start.3
  0.9 8.4 %copy-start = (f32[1,3,32,384]{3,2,1,0:T(8,128)S(1)}, f32[1,3,32,384]{3,2,1,0:T(8,128)}, u32[]{:S(2)}) copy-start(f32[1,3,32,384]{3,2,1,0:T(8,128)} %param.17) | copy-start | bytes 442372
  0.9 16.8 %collective-permute-start.2 = (f32[1,3,4,384]{3,2,1,0:T(4,128)S(1)}, f32[1,3,4,384]{3,2,1,0:T(4,128)S(1)}, u32[]{:S(2)}, u32[]{:S(2)}) collective-permute-start(f32[1,3,4,384]{3,2,1,0:T(4,128)S(1)} %get-tuple-element.413), channel_id=1, source_target_pairs={{0,1},{1,2},{2,3},{3,4},{4,5},{5,6},{6,7},{7,8},{8,9},{9,10},{10,1... | collective-permute-start | bytes 55304 | tf_op jit(solution)/shard_map/ppermute | solution.py:20
  5.1 12.6 %collective-permute-start.3 = (f32[1,3,4,384]{3,2,1,0:T(4,128)S(1)}, f32[1,3,4,384]{3,2,1,0:T(4,128)S(1)}, u32[]{:S(2)}, u32[]{:S(2)}) collective-permute-start(f32[1,3,4,384]{3,2,1,0:T(4,128)S(1)} %get-tuple-element.414), channel_id=1, source_target_pairs={{1,0},{2,1},{3,2},{4,3},{5,4},{6,5},{7,6},{8,7},{9,8},{10,9},{11,1... | collective-permute-start | bytes 55304 | tf_op jit(solution)/shard_map/ppermute | solution.py:23
  9.4 8.4 %collective-permute-start = (f32[1,3,4,384]{3,2,1,0:T(4,128)S(1)}, f32[1,3,4,384]{3,2,1,0:T(4,128)S(1)}, u32[]{:S(2)}, u32[]{:S(2)}) collective-permute-start(f32[1,3,4,384]{3,2,1,0:T(4,128)S(1)} %get-tuple-element.415), channel_id=1, source_target_pairs={{0,1},{1,2},{2,3},{3,4},{4,5},{5,6},{6,7},{7,8},{8,9},{9,10},{10,1... | collective-permute-start | bytes 55304 | tf_op jit(solution)/shard_map/ppermute | solution.py:20
  12.5 7.3 %collective-permute-start.1 = (f32[1,3,4,384]{3,2,1,0:T(4,128)S(1)}, f32[1,3,4,384]{3,2,1,0:T(4,128)S(1)}, u32[]{:S(2)}, u32[]{:S(2)}) collective-permute-start(f32[1,3,4,384]{3,2,1,0:T(4,128)S(1)} %get-tuple-element.416), channel_id=1, source_target_pairs={{1,0},{2,1},{3,2},{4,3},{5,4},{6,5},{7,6},{8,7},{9,8},{10,9},{11,1... | collective-permute-start | bytes 55304 | tf_op jit(solution)/shard_map/ppermute | solution.py:23
  24.4 8.3 %collective-permute-start.4 = (f32[1,3,4,384]{3,2,1,0:T(4,128)S(1)}, f32[1,3,4,384]{3,2,1,0:T(4,128)S(1)}, u32[]{:S(2)}, u32[]{:S(2)}) collective-permute-start(f32[1,3,4,384]{3,2,1,0:T(4,128)S(1)} %get-tuple-element.411), channel_id=1, source_target_pairs={{0,1},{1,2},{2,3},{3,4},{4,5},{5,6},{6,7},{7,8},{8,9},{9,10},{10,1... | collective-permute-start | bytes 55304 | tf_op jit(solution)/shard_map/ppermute | solution.py:20
  30.7 7.2 %collective-permute-start.5 = (f32[1,3,4,384]{3,2,1,0:T(4,128)S(1)}, f32[1,3,4,384]{3,2,1,0:T(4,128)S(1)}, u32[]{:S(2)}, u32[]{:S(2)}) collective-permute-start(f32[1,3,4,384]{3,2,1,0:T(4,128)S(1)} %get-tuple-element.412), channel_id=1, source_target_pairs={{1,0},{2,1},{3,2},{4,3},{5,4},{6,5},{7,6},{8,7},{9,8},{10,9},{11,1... | collective-permute-start | bytes 55304 | tf_op jit(solution)/shard_map/ppermute | solution.py:23
  42.5 8.3 %collective-permute-start.6 = (f32[1,3,4,384]{3,2,1,0:T(4,128)S(1)}, f32[1,3,4,384]{3,2,1,0:T(4,128)S(1)}, u32[]{:S(2)}, u32[]{:S(2)}) collective-permute-start(f32[1,3,4,384]{3,2,1,0:T(4,128)S(1)} %get-tuple-element.409), channel_id=1, source_target_pairs={{0,1},{1,2},{2,3},{3,4},{4,5},{5,6},{6,7},{7,8},{8,9},{9,10},{10,1... | collective-permute-start | bytes 55304 | tf_op jit(solution)/shard_map/ppermute | solution.py:20
  45.8 7.2 %collective-permute-start.7 = (f32[1,3,4,384]{3,2,1,0:T(4,128)S(1)}, f32[1,3,4,384]{3,2,1,0:T(4,128)S(1)}, u32[]{:S(2)}, u32[]{:S(2)}) collective-permute-start(f32[1,3,4,384]{3,2,1,0:T(4,128)S(1)} %get-tuple-element.410), channel_id=1, source_target_pairs={{1,0},{2,1},{3,2},{4,3},{5,4},{6,5},{7,6},{8,7},{9,8},{10,9},{11,1... | collective-permute-start | bytes 55304 | tf_op jit(solution)/shard_map/ppermute | solution.py:23
  57.5 2.2 %copy-start.1 = (f32[1,3,32,384]{3,2,1,0:T(8,128)S(1)}, f32[1,3,32,384]{3,2,1,0:T(8,128)}, u32[]{:S(2)}) copy-start(f32[1,3,32,384]{3,2,1,0:T(8,128)} %param.21) | copy-start | bytes 442372
  57.6 6.6 %copy-start.2 = (f32[1,3,32,384]{3,2,1,0:T(8,128)S(1)}, f32[1,3,32,384]{3,2,1,0:T(8,128)}, u32[]{:S(2)}) copy-start(f32[1,3,32,384]{3,2,1,0:T(8,128)} %param.20) | copy-start | bytes 442372
  57.6 6.6 %collective-permute-start.8 = (f32[1,3,32,384]{3,2,1,0:T(8,128)S(1)}, f32[1,3,32,384]{3,2,1,0:T(8,128)S(1)}, u32[]{:S(2)}, u32[]{:S(2)}) collective-permute-start(f32[1,3,32,384]{3,2,1,0:T(8,128)S(1)} %maximum_multiply_fusion.11), channel_id=1, source_target_pairs={{0,32},{32,64},{64,96},{96,128},{128,160},{160,192},{192,224},{224... | collective-permute-start | bytes 442376 | tf_op jit(solution)/shard_map/ppermute | solution.py:31
  129.2 4.6 %collective-permute-start.9 = (f32[1,3,32,384]{3,2,1,0:T(8,128)S(1)}, f32[1,3,32,384]{3,2,1,0:T(8,128)S(1)}, u32[]{:S(2)}, u32[]{:S(2)}) collective-permute-start(f32[1,3,32,384]{3,2,1,0:T(8,128)S(1)} %fusion.5), channel_id=1, source_target_pairs={{32,0},{64,32},{96,64},{128,96},{160,128},{192,160},{224,192},{256... | collective-permute-start | bytes 442376 | tf_op jit(solution)/shard_map/ppermute | solution.py:31
  139.0 8.9 %collective-permute-start.10 = (f32[1,3,4,384]{3,2,1,0:T(4,128)S(1)}, f32[1,3,4,384]{3,2,1,0:T(4,128)S(1)}, u32[]{:S(2)}, u32[]{:S(2)}) collective-permute-start(f32[1,3,4,384]{3,2,1,0:T(4,128)S(1)} %get-tuple-element.286), channel_id=1, source_target_pairs={{0,1},{1,2},{2,3},{3,4},{4,5},{5,6},{6,7},{7,8},{8,9},{9,10},{10,1... | collective-permute-start | bytes 55304 | tf_op jit(solution)/shard_map/ppermute | solution.py:20
  145.8 7.2 %collective-permute-start.11 = (f32[1,3,4,384]{3,2,1,0:T(4,128)S(1)}, f32[1,3,4,384]{3,2,1,0:T(4,128)S(1)}, u32[]{:S(2)}, u32[]{:S(2)}) collective-permute-start(f32[1,3,4,384]{3,2,1,0:T(4,128)S(1)} %get-tuple-element.285), channel_id=1, source_target_pairs={{1,0},{2,1},{3,2},{4,3},{5,4},{6,5},{7,6},{8,7},{9,8},{10,9},{11,1... | collective-permute-start | bytes 55304 | tf_op jit(solution)/shard_map/ppermute | solution.py:23
  158.2 8.3 %collective-permute-start.12 = (f32[1,3,4,384]{3,2,1,0:T(4,128)S(1)}, f32[1,3,4,384]{3,2,1,0:T(4,128)S(1)}, u32[]{:S(2)}, u32[]{:S(2)}) collective-permute-start(f32[1,3,4,384]{3,2,1,0:T(4,128)S(1)} %get-tuple-element.245), channel_id=1, source_target_pairs={{0,1},{1,2},{2,3},{3,4},{4,5},{5,6},{6,7},{7,8},{8,9},{9,10},{10,1... | collective-permute-start | bytes 55304 | tf_op jit(solution)/shard_map/ppermute | solution.py:20
  164.6 7.2 %collective-permute-start.13 = (f32[1,3,4,384]{3,2,1,0:T(4,128)S(1)}, f32[1,3,4,384]{3,2,1,0:T(4,128)S(1)}, u32[]{:S(2)}, u32[]{:S(2)}) collective-permute-start(f32[1,3,4,384]{3,2,1,0:T(4,128)S(1)} %get-tuple-element.244), channel_id=1, source_target_pairs={{1,0},{2,1},{3,2},{4,3},{5,4},{6,5},{7,6},{8,7},{9,8},{10,9},{11,1... | collective-permute-start | bytes 55304 | tf_op jit(solution)/shard_map/ppermute | solution.py:23
  177.0 8.3 %collective-permute-start.14 = (f32[1,3,4,384]{3,2,1,0:T(4,128)S(1)}, f32[1,3,4,384]{3,2,1,0:T(4,128)S(1)}, u32[]{:S(2)}, u32[]{:S(2)}) collective-permute-start(f32[1,3,4,384]{3,2,1,0:T(4,128)S(1)} %get-tuple-element.204), channel_id=1, source_target_pairs={{0,1},{1,2},{2,3},{3,4},{4,5},{5,6},{6,7},{7,8},{8,9},{9,10},{10,1... | collective-permute-start | bytes 55304 | tf_op jit(solution)/shard_map/ppermute | solution.py:20
  183.3 7.2 %collective-permute-start.15 = (f32[1,3,4,384]{3,2,1,0:T(4,128)S(1)}, f32[1,3,4,384]{3,2,1,0:T(4,128)S(1)}, u32[]{:S(2)}, u32[]{:S(2)}) collective-permute-start(f32[1,3,4,384]{3,2,1,0:T(4,128)S(1)} %get-tuple-element.203), channel_id=1, source_target_pairs={{1,0},{2,1},{3,2},{4,3},{5,4},{6,5},{7,6},{8,7},{9,8},{10,9},{11,1... | collective-permute-start | bytes 55304 | tf_op jit(solution)/shard_map/ppermute | solution.py:23
where the time goes:
time: 192 us; the launch traced here: 191 us
  blocking collectives  68.4 us (36%)
  starting transfers between devices  62.4 us (32%)
  waiting for transfers between devices  27.9 us (15%)
  local copies, waits for them, and re-layouts  16.2 us (8%)
  other arithmetic  14.4 us (8%)
  between operations  1.97 us (1%)
    all_gather x9, blocking collectives, prefix_by_axis(): pieces = jax.tree.map(lambda part: lax.all_gather(part, axis), total)  68.4 us
    ppermute x7, starting transfers between devices, with_halo(): lax.ppermute(lax.slice_in_dim(block, block.shape[dim] - width, None, axis...  36.3 us
    ppermute x7, waiting for transfers between devices, with_halo(): lax.ppermute(lax.slice_in_dim(block, 0, width, axis=dim), axis, backward)  24.8 us
    ppermute x7, starting transfers between devices, with_halo(): lax.ppermute(lax.slice_in_dim(block, 0, width, axis=dim), axis, backward)  22.2 us
    slice x94, local copies, waits for them, and re-layouts, along_x(): jnp.roll(field, 1, -1)  7.38 us
    another operation x36, other arithmetic, model_step(): return jnp.stack([new_height, new_east, new_north], axis=-3) * inside  4.17 us
    ppermute x2, starting transfers between devices, shifted(): lax.ppermute(value, axis, [(source, source + steps) for source in range(i...  3.97 us
  transfers between devices with their start and end apart: 16, of which 8 were waited for; matrix products, arithmetic and copies ran while one was open for 0% of the time, Pallas kernels for 0%

commit v1 on v0

v1 whole, which is shorter than its diff:
```python
import functools

import jax
import jax.numpy as jnp
from jax import lax
from jax.experimental import pallas as pl
from jax.experimental.pallas import tpu as pltpu
from jax.sharding import PartitionSpec as P

STEPS = 12
DT = 0.4
HALF = 0.5 * DT
LANES = 128
TOP = 24
MESH = pl.DeviceIdType.MESH


def lane_masks(shape):
    lane = lax.broadcasted_iota(jnp.int32, shape, len(shape) - 1)
    return lane == 0, lane == LANES - 1


def cycle(x, by):
    return jnp.concatenate([x[by:], x[:by]], axis=0)


def diff_x(f, masks):
    first, last = masks
    ahead = pltpu.roll(f, LANES - 1, 2)
    behind = pltpu.roll(f, 1, 2)
    return jnp.where(last, cycle(ahead, 1), ahead) - jnp.where(first, cycle(behind, -1), behind)


def tangent_step(src, dst, ref, tmp, fc, first, stop, keep_low, keep_high):
    cols = src.shape[0] // 3
    masks = lane_masks((cols, 8, LANES))
    for t in range(first - 1, stop + 1):
        rows = pl.ds(8 * t, 8)
        tmp[0:cols, rows] = (
            ref[0:cols, rows] * src[2 * cols :, rows] + ref[2 * cols :, rows] * src[0:cols, rows]
        )
    for t in range(first, stop):
        rows, below, above = (pl.ds(8 * t + d, 8) for d in (0, -1, 1))
        h, u, v = (src[i * cols : (i + 1) * cols, rows] for i in range(3))
        depth, east, north = (ref[i * cols : (i + 1) * cols, rows] for i in range(3))
        turn = fc[rows][None]

        def diff_y(buf, i):
            return buf[i * cols : (i + 1) * cols, above] - buf[i * cols : (i + 1) * cols, below]

        flux = depth * u + east * h
        new_h = h - (diff_x(flux, masks) + diff_y(tmp, 0))
        new_u = u - ((east * diff_x(u, masks) + north * diff_y(src, 1)) + (diff_x(h, masks) - turn * v))
        new_v = v - ((east * diff_x(v, masks) + north * diff_y(src, 2)) + (diff_y(src, 0) + turn * u))
        for i, new in enumerate((new_h, new_u, new_v)):
            if t == TOP // 8 - 1:
                new = jnp.where(keep_low, new, 0.0)
            if t == TOP // 8 + 4:
                new = jnp.where(keep_high, new, 0.0)
            dst[i * cols : (i + 1) * cols, rows] = new


def adjoint_step(src, dst, ref, tmp, fc, first, stop, keep_low, keep_high):
    cols = src.shape[0] // 3
    masks = lane_masks((cols, 8, LANES))
    for t in range(first - 1, stop + 1):
        rows = pl.ds(8 * t, 8)
        north = ref[2 * cols :, rows]
        tmp[0:cols, rows] = north * src[cols : 2 * cols, rows]
        tmp[cols : 2 * cols, rows] = north * src[2 * cols :, rows]
    for t in range(first, stop):
        rows, below, above = (pl.ds(8 * t + d, 8) for d in (0, -1, 1))
        p, q, s = (src[i * cols : (i + 1) * cols, rows] for i in range(3))
        depth, east, north = (ref[i * cols : (i + 1) * cols, rows] for i in range(3))
        turn = fc[rows][None]

        def diff_y(buf, i):
            return buf[i * cols : (i + 1) * cols, above] - buf[i * cols : (i + 1) * cols, below]

        px, py = diff_x(p, masks), diff_y(src, 0)
        new_p = p + ((east * px + north * py) + (diff_x(q, masks) + diff_y(src, 2)))
        new_q = q + ((depth * px - turn * s) + (diff_x(east * q, masks) + diff_y(tmp, 0)))
        new_s = s + ((depth * py + turn * q) + (diff_x(east * s, masks) + diff_y(tmp, 1)))
        for i, new in enumerate((new_p, new_q, new_s)):
            if t == TOP // 8 - 1:
                new = jnp.where(keep_low, new, 0.0)
            if t == TOP // 8 + 4:
                new = jnp.where(keep_high, new, 0.0)
            dst[i * cols : (i + 1) * cols, rows] = new


def run_steps(step, a, b):
    lo = TOP // 8
    step(a, b, lo - 2, lo + 6)
    step(b, a, lo - 2, lo + 6)
    step(a, b, lo - 2, lo + 6)

    def pair(_, carry):
        step(b, a, lo - 1, lo + 5)
        step(a, b, lo - 1, lo + 5)
        return carry

    lax.fori_loop(0, 4, pair, 0)
    step(b, a, lo, lo + 4)


def kernel(
    tms, strips, total_rows,
    inc_hbm, depth_hbm, wind_hbm, spread_hbm, decay_hbm, out_ref,
    fa, fb, ref, tmp, fc, spread, decay,
    halo_out, halo_in, pre_out, pre_in, tan_out, tan_in, scan_b, w_own, w_in, wl_in, wh_in, wk_in, wk,
    load_sem, halo_send, halo_recv, pre_send, pre_recv, tan_send, tan_recv,
    w_send, w_recv, wh_send, wl_recv, wh_recv, wk_send, wk_recv,
):
    nine = fa.shape[0]
    cols = nine // 3
    rows = spread.shape[1]
    per = rows // tms
    halo = STEPS
    edge = halo // per
    tm = lax.axis_index("tm")
    strip = lax.axis_index("strip")
    has_low, has_high = strip > 0, strip < strips - 1
    to_low, to_high = jnp.logical_and(has_low, tm < edge), jnp.logical_and(has_high, tm >= tms - edge)

    loads = []

    def load(hbm, planes, buf, base, offset, sem):
        for p in range(planes):
            for c in range(cols):
                copy = pltpu.make_async_copy(
                    hbm.at[0, p, :, pl.ds(c * LANES, LANES)],
                    buf.at[base + p * cols + c, pl.ds(offset, rows)],
                    load_sem.at[sem, p * cols + c],
                )
                copy.start()
                loads.append(copy)

    load(inc_hbm, 3, fa, 0, TOP, 0)
    load(depth_hbm, 1, ref, 0, TOP, 1)
    load(wind_hbm, 2, ref, cols, TOP, 2)
    load(spread_hbm, 3, spread, 0, 0, 3)
    load(decay_hbm, 3, decay, 0, 0, 4)

    barrier = pltpu.get_barrier_semaphore()
    for d in range(1, tms):
        pl.semaphore_signal(barrier, inc=1, device_id=(lax.rem(tm + d, tms), strip), device_id_type=MESH)

    @pl.when(has_low)
    def _():
        pl.semaphore_signal(barrier, inc=1, device_id=(tm, strip - 1), device_id_type=MESH)

    @pl.when(has_high)
    def _():
        pl.semaphore_signal(barrier, inc=1, device_id=(tm, strip + 1), device_id_type=MESH)

    for buf in (fa, fb, ref):
        buf[:, 0:TOP] = jnp.zeros((nine, TOP, LANES), jnp.float32)
        buf[:, TOP + rows :] = jnp.zeros((nine, fa.shape[1] - TOP - rows, LANES), jnp.float32)
    tmp[...] = jnp.zeros_like(tmp)
    row = lax.broadcasted_iota(jnp.int32, fc.shape, 0) + (strip * rows - TOP)
    fc[...] = DT * (0.2 + 0.4 * row.astype(jnp.float32) / total_rows)

    for copy in loads:
        copy.wait()

    for i in range(nine):
        for j in range(tms):
            pre_out[j, 2 * i : 2 * i + per] = fa[i, TOP + per * j : TOP + per * (j + 1)]
            pre_out[j, 18 + 2 * i : 18 + 2 * i + per] = spread[i, per * j : per * (j + 1)]
            pre_out[j, 36 + 2 * i : 36 + 2 * i + per] = decay[i, per * j : per * (j + 1)]

    own = pl.ds(TOP, rows)
    fa[0:cols, own] = fa[0:cols, own] * HALF
    ref[0:cols, own] = ref[0:cols, own] * (HALF * HALF)
    ref[cols:, own] = ref[cols:, own] * HALF

    for i in range(nine):
        for n, buf in ((0, fa), (nine, ref)):
            at = (n + i) * halo
            halo_out[0, at : at + halo] = buf[i, TOP : TOP + halo]
            halo_out[1, at : at + halo] = buf[i, TOP + rows - halo : TOP + rows]

    inside = jnp.logical_and(has_low, has_high)

    @pl.when(inside)
    def _():
        pl.semaphore_wait(barrier, tms + 1)

    @pl.when(jnp.logical_not(inside))
    def _():
        pl.semaphore_wait(barrier, tms)

    to_below = pltpu.make_async_remote_copy(
        halo_out.at[0], halo_in.at[1], halo_send.at[0], halo_recv.at[1],
        device_id=(tm, strip - 1), device_id_type=MESH,
    )
    to_above = pltpu.make_async_remote_copy(
        halo_out.at[1], halo_in.at[0], halo_send.at[1], halo_recv.at[0],
        device_id=(tm, strip + 1), device_id_type=MESH,
    )

    @pl.when(has_low)
    def _():
        to_below.start()

    @pl.when(has_high)
    def _():
        to_above.start()

    def spread_out(out, into, send, recv):
        copies = []
        for d in range(1, tms):
            to = lax.rem(tm + d, tms)
            copies.append(pltpu.make_async_remote_copy(
                out.at[to], into.at[tm], send.at[d], recv.at[tms - d],
                device_id=(to, strip), device_id_type=MESH,
            ))
        for copy in copies:
            copy.start()
        into[tm] = out[tm]
        return copies

    pre_copies = spread_out(pre_out, pre_in, pre_send, pre_recv)

    @pl.when(has_low)
    def _():
        to_above.wait_recv()
        for i in range(nine):
            for n, buf in ((0, fa), (nine, ref)):
                buf[i, TOP - halo : TOP] = halo_in[0, (n + i) * halo : (n + i + 1) * halo]

    @pl.when(has_high)
    def _():
        to_below.wait_recv()
        for i in range(nine):
            for n, buf in ((0, fa), (nine, ref)):
                buf[i, TOP + rows : TOP + rows + halo] = halo_in[1, (n + i) * halo : (n + i + 1) * halo]

    run_steps(
        lambda a, b, first, stop: tangent_step(a, b, ref, tmp, fc, first, stop, has_low, has_high), fa, fb
    )
    for i in range(nine):
        for j in range(tms):
            part = fa[i, TOP + per * j : TOP + per * (j + 1)]
            tan_out[j, per * i : per * (i + 1)] = part * (1.0 / HALF) if i < cols else part

    tan_copies = spread_out(tan_out, tan_in, tan_send, tan_recv)

    for copy in pre_copies:
        copy.wait_recv()
    for copy in tan_copies:
        copy.wait_recv()
    flat = per * nine
    built = None
    for k in range(tms):
        residual = pre_in[k, 0:flat]
        if k:
            residual = residual - tan_in[k - 1]
        scaled = pre_in[k, flat : 2 * flat] * residual
        built = scaled if k == 0 else pre_in[k, 2 * flat :] * built + scaled
        scan_b[k] = built
    w_own[tms] = jnp.zeros((flat, LANES), jnp.float32)
    smoothed = None
    for k in reversed(range(tms)):
        smoothed = scan_b[k] if smoothed is None else scan_b[k] + pre_in[k + 1, 2 * flat :] * smoothed
        w_own[k] = pre_in[k, flat : 2 * flat] * smoothed

    w_copies, low_copies, high_copies, wk_copies = [], [], [], []
    for d in range(tms):
        to = lax.rem(tm + d, tms)
        low_copies.append(pltpu.make_async_remote_copy(
            w_own.at[to + 1], wh_in.at[lax.rem(tm, edge)], wh_send.at[d], wh_recv.at[lax.rem(tm, edge)],
            device_id=(to, strip - 1), device_id_type=MESH,
        ))
        high_copies.append(pltpu.make_async_remote_copy(
            w_own.at[to + 1], wl_in.at[lax.rem(tm + edge - (tms - edge) % edge, edge)], wh_send.at[d],
            wl_recv.at[lax.rem(tm + edge - (tms - edge) % edge, edge)],
            device_id=(to, strip + 1), device_id_type=MESH,
        ))
        if d:
            w_copies.append(pltpu.make_async_remote_copy(
                w_own.at[to + 1], w_in.at[tm], w_send.at[d], w_recv.at[tms - d],
                device_id=(to, strip), device_id_type=MESH,
            ))
            wk_copies.append(pltpu.make_async_remote_copy(
                w_own.at[to], wk_in.at[tm], wk_send.at[d], wk_recv.at[tms - d],
                device_id=(to, strip), device_id_type=MESH,
            ))

    @pl.when(to_low)
    def _():
        for copy in low_copies:
            copy.start()

    @pl.when(to_high)
    def _():
        for copy in high_copies:
            copy.start()

    for copy in w_copies:
        copy.start()
    for copy in wk_copies:
        copy.start()
    w_in[tm] = w_own[tm + 1]
    wk_in[tm] = w_own[tm]

    @pl.when(jnp.logical_not(has_low))
    def _():
        fa[:, 0:TOP] = jnp.zeros((nine, TOP, LANES), jnp.float32)

    @pl.when(jnp.logical_not(has_high))
    def _():
        fa[:, TOP + rows :] = jnp.zeros((nine, fa.shape[1] - TOP - rows, LANES), jnp.float32)

    def unpack(slab, at):
        for i in range(nine):
            part = slab[per * i : per * (i + 1)]
            fa[i, at : at + per] = part * (1.0 / HALF) if i < cols else part

    for copy in w_copies:
        copy.wait_recv()
    for j in range(tms):
        unpack(w_in.at[j], TOP + per * j)

    @pl.when(has_low)
    def _():
        for q in range(edge):
            pltpu.make_async_copy(wl_in.at[q], wl_in.at[q], wl_recv.at[q]).wait()
            unpack(wl_in.at[q], TOP - halo + per * q)

    @pl.when(has_high)
    def _():
        for q in range(edge):
            pltpu.make_async_copy(wh_in.at[q], wh_in.at[q], wh_recv.at[q]).wait()
            unpack(wh_in.at[q], TOP + rows + per * q)

    run_steps(
        lambda a, b, first, stop: adjoint_step(a, b, ref, tmp, fc, first, stop, has_low, has_high), fa, fb
    )
    for copy in wk_copies:
        copy.wait_recv()
    for j in range(tms):
        for i in range(nine):
            wk[i, per * j : per * (j + 1)] = wk_in[j, per * i : per * (i + 1)]
    for i in range(nine):
        adjoint = fa[i, own]
        if i < cols:
            adjoint = adjoint * HALF
        out_ref[0, i // cols, :, (i % cols) * LANES : (i % cols + 1) * LANES] = wk[i] - adjoint

    @pl.when(has_low)
    def _():
        to_below.wait_send()

    @pl.when(has_high)
    def _():
        to_above.wait_send()

    @pl.when(to_low)
    def _():
        for copy in low_copies:
            copy.wait_send()

    @pl.when(to_high)
    def _():
        for copy in high_copies:
            copy.wait_send()

    for copy in pre_copies + tan_copies + w_copies + wk_copies:
        copy.wait_send()


def body(tms, strips, increment, ref_depth, ref_wind, spread, decay):
    _, planes, rows, width = increment.shape
    cols = width // LANES
    nine = planes * cols
    per = rows // tms
    flat = per * nine
    edge = STEPS // per
    height = rows + 2 * TOP
    dma = pltpu.SemaphoreType.DMA
    f32 = jnp.float32
    vmem = lambda *shape: pltpu.VMEM(shape, f32)
    hbm = pl.BlockSpec(memory_space=pl.ANY)
    return pl.pallas_call(
        functools.partial(kernel, tms, strips, strips * rows),
        out_shape=jax.ShapeDtypeStruct(increment.shape, f32),
        in_specs=[hbm] * 5,
        out_specs=pl.BlockSpec(memory_space=pltpu.VMEM),
        scratch_shapes=[
            vmem(nine, height, LANES), vmem(nine, height, LANES), vmem(nine, height, LANES),
            vmem(2 * cols, height, LANES), vmem(height, LANES),
            vmem(nine, rows, LANES), vmem(nine, rows, LANES),
            vmem(2, 2 * nine * STEPS, LANES), vmem(2, 2 * nine * STEPS, LANES),
            vmem(tms, 3 * flat, LANES), vmem(tms, 3 * flat, LANES),
            vmem(tms, flat, LANES), vmem(tms, flat, LANES),
            vmem(tms, flat, LANES), vmem(tms + 1, flat, LANES), vmem(tms, flat, LANES),
            vmem(edge, flat, LANES), vmem(edge, flat, LANES), vmem(tms, flat, LANES),
            vmem(nine, rows, LANES),
            dma((5, nine)), dma((2,)), dma((2,)),
            dma((tms,)), dma((tms,)), dma((tms,)), dma((tms,)),
            dma((tms,)), dma((tms,)), dma((tms,)), dma((edge,)), dma((edge,)), dma((tms,)), dma((tms,)),
        ],
        compiler_params=pltpu.CompilerParams(collective_id=0, has_side_effects=True),
    )(increment, ref_depth, ref_wind, spread, decay)


def solution(mesh):
    spec = P("tm", None, "strip", None)
    return jax.shard_map(
        functools.partial(body, mesh.shape["tm"], mesh.shape["strip"]),
        mesh=mesh,
        in_specs=(spec,) * 5,
        out_specs=spec,
        check_vma=False,
    )
```

time: 192 us -> 34.7 us (0.18)
  the two profiles are of different devices: /device:TPU:162 before, /device:TPU:393 now
where the time goes in v1:
time: 34.7 us; the launch traced here: 34.5 us
  Pallas kernels  32.9 us (95%)
  local copies, waits for them, and re-layouts  1.58 us (5%)
    pallas_call x1, Pallas kernels, body(): pl.pallas_call(functools.partial(kernel, tms, strips, strips * rows), out...  32.9 us
    unnamed x1, local copies, waits for them, and re-layouts  1.58 us

profile of v1, /device:TPU:393, one launch (start us, length us, event | category | flops | bytes accessed | tf_op | source)
XLA Modules:
  0.0 34.5 jit_solution(10740343326028133737)
XLA Ops:
  0.0 32.9 %shard_map.55 = f32[1,3,32,384]{3,2,1,0:T(8,128)} custom-call(f32[1,3,32,384]{3,2,1,0:T(8,128)} %inc_hbm.1, f32[1,1,32,384]{3,2,1,0:T(8,128)} %depth_hbm.1, f32[1,2,32,384]{3,2,1,0:T(8,128)} %wind_hbm.1, f32[1,3,32,384]{3,2,1,0:T(8,128)} %spread_hbm.1, f32[1,3,32,384]{3,2,1,0:T(8,128)} %decay_hbm.1), custom_call_target="tpu_custom_call" | custom-call | tf_op jit(solution)/shard_map/pallas_call | solution.py:386
  32.9 1.6 %copy.7 = f32[1,3,32,384]{3,2,1,0:T(8,128)} copy(f32[1,3,32,384]{3,2,1,0:T(8,128)} %shard_map.55) | data formatting | bytes 294912

commit v2 on v1

v2 whole, which is shorter than its diff:
```python
import functools

import jax
import jax.numpy as jnp
from jax import lax
from jax.experimental import pallas as pl
from jax.experimental.pallas import tpu as pltpu
from jax.sharding import PartitionSpec as P

STEPS = 12
DT = 0.4
HALF = 0.5 * DT
LANES = 128
TOP = 24
MESH = pl.DeviceIdType.MESH


def diff_x(f):
    after = pltpu.roll(f[:1], LANES - 1, 2)
    before = pltpu.roll(f[-1:], 1, 2)
    return jnp.concatenate([f[1:], after], axis=0) - jnp.concatenate([before, f[:-1]], axis=0)


def third(x):
    return (x * 21846) >> 16


def column_maps(cols):
    lane = lax.broadcasted_iota(jnp.int32, (8, LANES), 1)
    rest = lane - cols * third(lane)
    into, back = [], []
    for j in range(cols):
        x = cols * lane + j
        into.append(x & (LANES - 1))
        block = rest + 2 * j
        block = block - cols * third(block)
        back.append(third(LANES * block + lane - j))
    return (rest == 0, rest == 1), into, back


def choose(marks, parts, j):
    pick = [parts[(2 * j + r) % len(parts)] for r in range(3)]
    return jnp.where(marks[0], pick[0], jnp.where(marks[1], pick[1], pick[2]))


def take_lanes(x, index):
    return jnp.take_along_axis(x, index, axis=1, mode="promise_in_bounds")


def tangent_step(src, dst, ref, tmp, fc, first, stop, keep_low, keep_high):
    cols = src.shape[0] // 3
    for t in range(first - 1, stop + 1):
        rows = pl.ds(8 * t, 8)
        tmp[0:cols, rows] = (
            ref[0:cols, rows] * src[2 * cols :, rows] + ref[2 * cols :, rows] * src[0:cols, rows]
        )
    for t in range(first, stop):
        rows, below, above = (pl.ds(8 * t + d, 8) for d in (0, -1, 1))
        h, u, v = (src[i * cols : (i + 1) * cols, rows] for i in range(3))
        depth, east, north = (ref[i * cols : (i + 1) * cols, rows] for i in range(3))
        turn = fc[rows][None]

        def diff_y(buf, i):
            return buf[i * cols : (i + 1) * cols, above] - buf[i * cols : (i + 1) * cols, below]

        flux = depth * u + east * h
        new_h = h - (diff_x(flux) + diff_y(tmp, 0))
        new_u = u - ((east * diff_x(u) + north * diff_y(src, 1)) + (diff_x(h) - turn * v))
        new_v = v - ((east * diff_x(v) + north * diff_y(src, 2)) + (diff_y(src, 0) + turn * u))
        for i, new in enumerate((new_h, new_u, new_v)):
            if t == TOP // 8 - 1:
                new = jnp.where(keep_low, new, 0.0)
            if t == TOP // 8 + 4:
                new = jnp.where(keep_high, new, 0.0)
            dst[i * cols : (i + 1) * cols, rows] = new


def adjoint_step(src, dst, ref, tmp, fc, first, stop, keep_low, keep_high):
    cols = src.shape[0] // 3
    for t in range(first - 1, stop + 1):
        rows = pl.ds(8 * t, 8)
        north = ref[2 * cols :, rows]
        tmp[0:cols, rows] = north * src[cols : 2 * cols, rows]
        tmp[cols : 2 * cols, rows] = north * src[2 * cols :, rows]
    for t in range(first, stop):
        rows, below, above = (pl.ds(8 * t + d, 8) for d in (0, -1, 1))
        p, q, s = (src[i * cols : (i + 1) * cols, rows] for i in range(3))
        depth, east, north = (ref[i * cols : (i + 1) * cols, rows] for i in range(3))
        turn = fc[rows][None]

        def diff_y(buf, i):
            return buf[i * cols : (i + 1) * cols, above] - buf[i * cols : (i + 1) * cols, below]

        px, py = diff_x(p), diff_y(src, 0)
        new_p = p + ((east * px + north * py) + (diff_x(q) + diff_y(src, 2)))
        new_q = q + ((depth * px - turn * s) + (diff_x(east * q) + diff_y(tmp, 0)))
        new_s = s + ((depth * py + turn * q) + (diff_x(east * s) + diff_y(tmp, 1)))
        for i, new in enumerate((new_p, new_q, new_s)):
            if t == TOP // 8 - 1:
                new = jnp.where(keep_low, new, 0.0)
            if t == TOP // 8 + 4:
                new = jnp.where(keep_high, new, 0.0)
            dst[i * cols : (i + 1) * cols, rows] = new


def run_steps(step, a, b):
    lo = TOP // 8
    step(a, b, lo - 2, lo + 6)
    step(b, a, lo - 2, lo + 6)
    step(a, b, lo - 2, lo + 6)

    def pair(_, carry):
        step(b, a, lo - 1, lo + 5)
        step(a, b, lo - 1, lo + 5)
        return carry

    lax.fori_loop(0, 4, pair, 0)
    step(b, a, lo, lo + 4)


def kernel(
    tms, strips, total_rows,
    inc_hbm, depth_hbm, wind_hbm, spread_hbm, decay_hbm, out_ref,
    raw, fa, fb, ref, tmp, fc, spread, decay,
    halo_out, halo_in, pre_out, pre_in, tan_out, tan_in, scan_b, w_own, w_in, wl_in, wh_in, wk_in, wk,
    load_sem, halo_send, halo_recv, pre_send, pre_recv, tan_send, tan_recv,
    w_send, w_recv, wh_send, wl_recv, wh_recv, wk_send, wk_recv,
):
    nine = fa.shape[0]
    cols = nine // 3
    rows = spread.shape[1]
    per = rows // tms
    halo = STEPS
    edge = halo // per
    tm = lax.axis_index("tm")
    strip = lax.axis_index("strip")
    has_low, has_high = strip > 0, strip < strips - 1
    to_low, to_high = jnp.logical_and(has_low, tm < edge), jnp.logical_and(has_high, tm >= tms - edge)

    barrier = pltpu.get_barrier_semaphore()

    @pl.when(has_low)
    def _():
        pl.semaphore_signal(barrier, inc=1, device_id=(tm, strip - 1), device_id_type=MESH)

    @pl.when(has_high)
    def _():
        pl.semaphore_signal(barrier, inc=1, device_id=(tm, strip + 1), device_id_type=MESH)

    for d in range(1, tms):
        pl.semaphore_signal(barrier, inc=1, device_id=(lax.rem(tm + d, tms), strip), device_id_type=MESH)

    loads = [
        pltpu.make_async_copy(hbm.at[0], buf, load_sem.at[n])
        for n, (hbm, buf) in enumerate((
            (inc_hbm, raw.at[0]), (depth_hbm, raw.at[1, 0:1]), (wind_hbm, raw.at[1, 1:3]),
            (spread_hbm, raw.at[2]), (decay_hbm, raw.at[3]),
        ))
    ]
    for copy in loads:
        copy.start()

    marks, into, back = column_maps(cols)
    own = pl.ds(TOP, rows)

    def regroup(n, p, buf, offset, scale):
        for t in range(rows // 8):
            at = pl.ds(8 * t, 8)
            parts = [raw[n, p, at, c * LANES : (c + 1) * LANES] for c in range(cols)]
            for j in range(cols):
                new = take_lanes(choose(marks, parts, j), into[j])
                buf[p * cols + j, pl.ds(offset + 8 * t, 8)] = new * scale if scale else new

    @pl.when(jnp.logical_not(has_low))
    def _():
        for buf in (fa, ref):
            buf[:, TOP - 16 : TOP] = jnp.zeros((nine, 16, LANES), jnp.float32)

    @pl.when(jnp.logical_not(has_high))
    def _():
        for buf in (fa, ref):
            buf[:, TOP + rows : TOP + rows + 16] = jnp.zeros((nine, 16, LANES), jnp.float32)

    row = lax.broadcasted_iota(jnp.int32, fc.shape, 0) + (strip * rows - TOP)
    fc[...] = DT * (0.2 + 0.4 * row.astype(jnp.float32) / total_rows)

    loads[0].wait()
    for p in range(3):
        regroup(0, p, fa, TOP, HALF if p == 0 else None)
    loads[1].wait()
    loads[2].wait()
    for p in range(3):
        regroup(1, p, ref, TOP, HALF * HALF if p == 0 else HALF)

    for i in range(nine):
        for n, buf in ((0, fa), (nine, ref)):
            at = (n + i) * halo
            halo_out[0, at : at + halo] = buf[i, TOP : TOP + halo]
            halo_out[1, at : at + halo] = buf[i, TOP + rows - halo : TOP + rows]

    inside = jnp.logical_and(has_low, has_high)

    @pl.when(inside)
    def _():
        pl.semaphore_wait(barrier, tms + 1)

    @pl.when(jnp.logical_not(inside))
    def _():
        pl.semaphore_wait(barrier, tms)

    to_below = pltpu.make_async_remote_copy(
        halo_out.at[0], halo_in.at[1], halo_send.at[0], halo_recv.at[1],
        device_id=(tm, strip - 1), device_id_type=MESH,
    )
    to_above = pltpu.make_async_remote_copy(
        halo_out.at[1], halo_in.at[0], halo_send.at[1], halo_recv.at[0],
        device_id=(tm, strip + 1), device_id_type=MESH,
    )

    @pl.when(has_low)
    def _():
        to_below.start()

    @pl.when(has_high)
    def _():
        to_above.start()

    def wait_for(slabs, sem):
        pltpu.make_async_copy(slabs, slabs, sem).wait()

    def spread_out(out, into, send, recv):
        copies = []
        for d in range(1, tms):
            to = lax.rem(tm + d, tms)
            copies.append(pltpu.make_async_remote_copy(
                out.at[to], into.at[tm], send, recv,
                device_id=(to, strip), device_id_type=MESH,
            ))
        for copy in copies:
            copy.start()
        into[tm] = out[tm]

    for n, buf in ((2, spread), (3, decay)):
        loads[n + 1].wait()
        for p in range(3):
            regroup(n, p, buf, 0, None)
    for i in range(nine):
        for j in range(tms):
            here = slice(per * j, per * (j + 1))
            for n, part in enumerate((fa[i, TOP + per * j : TOP + per * (j + 1)], spread[i, here], decay[i, here])):
                at = per * (n * nine + i)
                pre_out[j, at : at + per] = part
    spread_out(pre_out, pre_in, pre_send, pre_recv)

    @pl.when(has_low)
    def _():
        to_above.wait_recv()
        for i in range(nine):
            for n, buf in ((0, fa), (nine, ref)):
                buf[i, TOP - halo : TOP] = halo_in[0, (n + i) * halo : (n + i + 1) * halo]

    @pl.when(has_high)
    def _():
        to_below.wait_recv()
        for i in range(nine):
            for n, buf in ((0, fa), (nine, ref)):
                buf[i, TOP + rows : TOP + rows + halo] = halo_in[1, (n + i) * halo : (n + i + 1) * halo]

    run_steps(
        lambda a, b, first, stop: tangent_step(a, b, ref, tmp, fc, first, stop, has_low, has_high), fa, fb
    )
    for i in range(nine):
        for j in range(tms):
            tan_out[j, per * i : per * (i + 1)] = fa[i, TOP + per * j : TOP + per * (j + 1)]

    spread_out(tan_out, tan_in, tan_send, tan_recv)

    others = pl.ds(0, tms - 1)
    wait_for(pre_in.at[others], pre_recv)
    wait_for(tan_in.at[others], tan_recv)
    flat = per * nine
    built = None
    for k in range(tms):
        residual = pre_in[k, 0:flat]
        if k:
            residual = residual - tan_in[k - 1]
        scaled = pre_in[k, flat : 2 * flat] * residual
        built = scaled if k == 0 else pre_in[k, 2 * flat :] * built + scaled
        scan_b[k] = built
    w_own[tms] = jnp.zeros((flat, LANES), jnp.float32)
    smoothed = None
    for k in reversed(range(tms)):
        smoothed = scan_b[k] if smoothed is None else scan_b[k] + pre_in[k + 1, 2 * flat :] * smoothed
        w_own[k] = pre_in[k, flat : 2 * flat] * smoothed

    w_copies, low_copies, high_copies, wk_copies = [], [], [], []
    for d in range(tms):
        to = lax.rem(tm + d, tms)
        low_copies.append(pltpu.make_async_remote_copy(
            w_own.at[to + 1], wh_in.at[lax.rem(tm, edge)], wh_send, wh_recv,
            device_id=(to, strip - 1), device_id_type=MESH,
        ))
        high_copies.append(pltpu.make_async_remote_copy(
            w_own.at[to + 1], wl_in.at[lax.rem(tm + edge - (tms - edge) % edge, edge)], wh_send, wl_recv,
            device_id=(to, strip + 1), device_id_type=MESH,
        ))
        if d:
            w_copies.append(pltpu.make_async_remote_copy(
                w_own.at[to + 1], w_in.at[tm], w_send, w_recv,
                device_id=(to, strip), device_id_type=MESH,
            ))
            wk_copies.append(pltpu.make_async_remote_copy(
                w_own.at[to], wk_in.at[tm], wk_send, wk_recv,
                device_id=(to, strip), device_id_type=MESH,
            ))

    @pl.when(to_low)
    def _():
        for copy in low_copies:
            copy.start()

    @pl.when(to_high)
    def _():
        for copy in high_copies:
            copy.start()

    for copy in w_copies:
        copy.start()
    for copy in wk_copies:
        copy.start()
    w_in[tm] = w_own[tm + 1]
    wk_in[tm] = w_own[tm]

    @pl.when(jnp.logical_not(has_low))
    def _():
        fa[:, TOP - 16 : TOP] = jnp.zeros((nine, 16, LANES), jnp.float32)

    @pl.when(jnp.logical_not(has_high))
    def _():
        fa[:, TOP + rows : TOP + rows + 16] = jnp.zeros((nine, 16, LANES), jnp.float32)

    def unpack(slab, at):
        for i in range(nine):
            part = slab[per * i : per * (i + 1)]
            fa[i, at : at + per] = part * (1.0 / HALF**2) if i < cols else part

    wait_for(w_in.at[others], w_recv)
    for j in range(tms):
        unpack(w_in.at[j], TOP + per * j)

    @pl.when(has_low)
    def _():
        wait_for(wl_in, wl_recv)
        for q in range(edge):
            unpack(wl_in.at[q], TOP - halo + per * q)

    @pl.when(has_high)
    def _():
        wait_for(wh_in, wh_recv)
        for q in range(edge):
            unpack(wh_in.at[q], TOP + rows + per * q)

    run_steps(
        lambda a, b, first, stop: adjoint_step(a, b, ref, tmp, fc, first, stop, has_low, has_high), fa, fb
    )
    wait_for(wk_in.at[others], wk_recv)
    for j in range(tms):
        for i in range(nine):
            wk[i, per * j : per * (j + 1)] = wk_in[j, per * i : per * (i + 1)]
    for p in range(3):
        for t in range(rows // 8):
            at = pl.ds(8 * t, 8)
            parts = []
            for j in range(cols):
                weighted, adjoint = wk[p * cols + j, at], fa[p * cols + j, pl.ds(TOP + 8 * t, 8)]
                if p == 0:
                    weighted, adjoint = weighted * (1.0 / HALF), adjoint * HALF
                parts.append(take_lanes(weighted - adjoint, back[j]))
            for c in range(cols):
                out_ref[0, p, at, c * LANES : (c + 1) * LANES] = choose(marks, parts, c)

    @pl.when(has_low)
    def _():
        to_below.wait_send()

    @pl.when(has_high)
    def _():
        to_above.wait_send()

    @pl.when(jnp.logical_or(to_low, to_high))
    def _():
        wait_for(w_own.at[pl.ds(0, tms)], wh_send)

    for slabs, sem in ((pre_out, pre_send), (tan_out, tan_send), (w_own, w_send), (w_own, wk_send)):
        wait_for(slabs.at[others], sem)


def body(tms, strips, increment, ref_depth, ref_wind, spread, decay):
    _, planes, rows, width = increment.shape
    cols = width // LANES
    nine = planes * cols
    per = rows // tms
    flat = per * nine
    edge = STEPS // per
    height = rows + 2 * TOP
    dma = pltpu.SemaphoreType.DMA
    f32 = jnp.float32
    vmem = lambda *shape: pltpu.VMEM(shape, f32)
    hbm = pl.BlockSpec(memory_space=pl.ANY)
    return pl.pallas_call(
        functools.partial(kernel, tms, strips, strips * rows),
        out_shape=jax.ShapeDtypeStruct(increment.shape, f32),
        in_specs=[hbm] * 5,
        out_specs=pl.BlockSpec(memory_space=pltpu.VMEM),
        scratch_shapes=[
            vmem(4, planes, rows, width),
            vmem(nine, height, LANES), vmem(nine, height, LANES), vmem(nine, height, LANES),
            vmem(2 * cols, height, LANES), vmem(height, LANES),
            vmem(nine, rows, LANES), vmem(nine, rows, LANES),
            vmem(2, 2 * nine * STEPS, LANES), vmem(2, 2 * nine * STEPS, LANES),
            vmem(tms, 3 * flat, LANES), vmem(tms, 3 * flat, LANES),
            vmem(tms, flat, LANES), vmem(tms, flat, LANES),
            vmem(tms, flat, LANES), vmem(tms + 1, flat, LANES), vmem(tms, flat, LANES),
            vmem(edge, flat, LANES), vmem(edge, flat, LANES), vmem(tms, flat, LANES),
            vmem(nine, rows, LANES),
            dma((5,)), dma((2,)), dma((2,)), *[dma] * 11,
        ],
        compiler_params=pltpu.CompilerParams(
            collective_id=0, has_side_effects=True, vmem_limit_bytes=24 * 2**20
        ),
    )(*(pltpu.with_memory_space_constraint(x, pltpu.HBM) for x in (increment, ref_depth, ref_wind, spread, decay)))


def solution(mesh):
    spec = P("tm", None, "strip", None)
    return jax.shard_map(
        functools.partial(body, mesh.shape["tm"], mesh.shape["strip"]),
        mesh=mesh,
        in_specs=(spec,) * 5,
        out_specs=spec,
        check_vma=False,
    )
```

time: 34.7 us -> 30 us (0.86)
  the two profiles are of different devices: /device:TPU:393 before, /device:TPU:385 now
where the time goes in v2:
time: 30 us; the launch traced here: 29.9 us
  Pallas kernels  29.2 us (97%)
  local copies, waits for them, and re-layouts  0.66 us (2%)
    pallas_call x1, Pallas kernels, body(): pl.pallas_call(functools.partial(kernel, tms, strips, strips * rows), out...  29.2 us
    unnamed x1, local copies, waits for them, and re-layouts  0.66 us

profile of v2, /device:TPU:385, one launch (start us, length us, event | category | flops | bytes accessed | tf_op | source)
XLA Modules:
  0.0 29.9 jit_solution(2160436757537966769)
XLA Ops:
  0.0 29.2 %shard_map.55 = f32[1,3,32,384]{3,2,1,0:T(8,128)S(1)} custom-call(f32[1,3,32,384]{3,2,1,0:T(8,128)} %inc_hbm.1, f32[1,1,32,384]{3,2,1,0:T(8,128)} %depth_hbm.1, f32[1,2,32,384]{3,2,1,0:T(8,128)} %wind_hbm.1, f32[1,3,32,384]{3,2,1,0:T(8,128)} %spread_hbm.1, f32[1,3,32,384]{3,2,1,0:T(8,128)} %decay_hbm.1), custom_call_target="tpu_custom_call" | custom-call | tf_op jit(solution)/shard_map/pallas_call | solution.py:410
  29.2 0.7 %copy.7 = f32[1,3,32,384]{3,2,1,0:T(8,128)} copy(f32[1,3,32,384]{3,2,1,0:T(8,128)S(1)} %shard_map.55) | data formatting | bytes 294912

commit v3 on v2

--- a/solution.py
+++ b/solution.py
@@ -13,6 +13,9 @@
 LANES = 128
 TOP = 24
 MESH = pl.DeviceIdType.MESH
+ORDER = [(dy, dx, dc) for dx in (0, 1) for dy in (2, 1, 3, 0) for dc in (0, 1)]
+NEAR, FAR = ORDER[:8], ORDER[8:]
+RETURN = ((FAR, NEAR), (NEAR, FAR))
 
 
 def diff_x(f):
@@ -47,95 +50,114 @@
     return jnp.take_along_axis(x, index, axis=1, mode="promise_in_bounds")
 
 
-def tangent_step(src, dst, ref, tmp, fc, first, stop, keep_low, keep_high):
+def tangent_products(new, ref, rows, tmp):
+    cols = tmp.shape[0] // 2
+    tmp[:cols, rows] = ref[0:cols, rows] * new[2] + ref[2 * cols :, rows] * new[0]
+
+
+def tangent_tile(src, ref, tmp, fc, at):
     cols = src.shape[0] // 3
-    for t in range(first - 1, stop + 1):
-        rows = pl.ds(8 * t, 8)
-        tmp[0:cols, rows] = (
-            ref[0:cols, rows] * src[2 * cols :, rows] + ref[2 * cols :, rows] * src[0:cols, rows]
-        )
-    for t in range(first, stop):
-        rows, below, above = (pl.ds(8 * t + d, 8) for d in (0, -1, 1))
-        h, u, v = (src[i * cols : (i + 1) * cols, rows] for i in range(3))
-        depth, east, north = (ref[i * cols : (i + 1) * cols, rows] for i in range(3))
-        turn = fc[rows][None]
-
-        def diff_y(buf, i):
-            return buf[i * cols : (i + 1) * cols, above] - buf[i * cols : (i + 1) * cols, below]
-
-        flux = depth * u + east * h
-        new_h = h - (diff_x(flux) + diff_y(tmp, 0))
-        new_u = u - ((east * diff_x(u) + north * diff_y(src, 1)) + (diff_x(h) - turn * v))
-        new_v = v - ((east * diff_x(v) + north * diff_y(src, 2)) + (diff_y(src, 0) + turn * u))
-        for i, new in enumerate((new_h, new_u, new_v)):
-            if t == TOP // 8 - 1:
-                new = jnp.where(keep_low, new, 0.0)
-            if t == TOP // 8 + 4:
-                new = jnp.where(keep_high, new, 0.0)
-            dst[i * cols : (i + 1) * cols, rows] = new
-
-
-def adjoint_step(src, dst, ref, tmp, fc, first, stop, keep_low, keep_high):
+    rows, below, above = (pl.ds(at + d, 8) for d in (0, -1, 1))
+
+    def diff_y(buf, i):
+        return buf[i * cols : (i + 1) * cols, above] - buf[i * cols : (i + 1) * cols, below]
+
+    h, u, v = (src[i * cols : (i + 1) * cols, rows] for i in range(3))
+    depth, east, north = (ref[i * cols : (i + 1) * cols, rows] for i in range(3))
+    turn = fc[rows][None]
+    flux = depth * u + east * h
+    new_h = h - (diff_x(flux) + diff_y(tmp, 0))
+    new_u = u - ((east * diff_x(u) + north * diff_y(src, 1)) + (diff_x(h) - turn * v))
+    new_v = v - ((east * diff_x(v) + north * diff_y(src, 2)) + (diff_y(src, 0) + turn * u))
+    return new_h, new_u, new_v
+
+
+def adjoint_products(new, ref, rows, tmp):
+    cols = tmp.shape[0] // 2
+    north = ref[2 * cols :, rows]
+    tmp[:cols, rows] = north * new[1]
+    tmp[cols:, rows] = north * new[2]
+
+
+def adjoint_tile(src, ref, tmp, fc, at):
     cols = src.shape[0] // 3
-    for t in range(first - 1, stop + 1):
-        rows = pl.ds(8 * t, 8)
-        north = ref[2 * cols :, rows]
-        tmp[0:cols, rows] = north * src[cols : 2 * cols, rows]
-        tmp[cols : 2 * cols, rows] = north * src[2 * cols :, rows]
-    for t in range(first, stop):
-        rows, below, above = (pl.ds(8 * t + d, 8) for d in (0, -1, 1))
-        p, q, s = (src[i * cols : (i + 1) * cols, rows] for i in range(3))
-        depth, east, north = (ref[i * cols : (i + 1) * cols, rows] for i in range(3))
-        turn = fc[rows][None]
-
-        def diff_y(buf, i):
-            return buf[i * cols : (i + 1) * cols, above] - buf[i * cols : (i + 1) * cols, below]
-
-        px, py = diff_x(p), diff_y(src, 0)
-        new_p = p + ((east * px + north * py) + (diff_x(q) + diff_y(src, 2)))
-        new_q = q + ((depth * px - turn * s) + (diff_x(east * q) + diff_y(tmp, 0)))
-        new_s = s + ((depth * py + turn * q) + (diff_x(east * s) + diff_y(tmp, 1)))
-        for i, new in enumerate((new_p, new_q, new_s)):
-            if t == TOP // 8 - 1:
-                new = jnp.where(keep_low, new, 0.0)
-            if t == TOP // 8 + 4:
-                new = jnp.where(keep_high, new, 0.0)
-            dst[i * cols : (i + 1) * cols, rows] = new
-
-
-def run_steps(step, a, b):
-    lo = TOP // 8
-    step(a, b, lo - 2, lo + 6)
-    step(b, a, lo - 2, lo + 6)
-    step(a, b, lo - 2, lo + 6)
+    rows, below, above = (pl.ds(at + d, 8) for d in (0, -1, 1))
+
+    def diff_y(buf, i):
+        return buf[i * cols : (i + 1) * cols, above] - buf[i * cols : (i + 1) * cols, below]
+
+    p, q, s = (src[i * cols : (i + 1) * cols, rows] for i in range(3))
+    depth, east, north = (ref[i * cols : (i + 1) * cols, rows] for i in range(3))
+    turn = fc[rows][None]
+    px, py = diff_x(p), diff_y(src, 0)
+    new_p = p + ((east * px + north * py) + (diff_x(q) + diff_y(src, 2)))
+    new_q = q + ((depth * px - turn * s) + (diff_x(east * q) + diff_y(tmp, 0)))
+    new_s = s + ((depth * py + turn * q) + (diff_x(east * s) + diff_y(tmp, 1)))
+    return new_p, new_q, new_s
+
+
+def run_steps(tile, products, bufs, ref, fc, rows, has_low, has_high):
+    lo, hi = TOP // 8, (TOP + rows) // 8
+    cols = ref.shape[0] // 3
+
+    for t in range(lo - 2, hi + 2):
+        at = pl.ds(8 * t, 8)
+        products([bufs[0][0][i * cols : (i + 1) * cols, at] for i in range(3)], ref, at, bufs[0][1])
+
+    def step(j, more, last=False):
+        (src, tmp), (dst, new_tmp) = bufs if j % 2 else bufs[::-1]
+        for t in range(lo - more, hi + more):
+            new = tile(src, ref, tmp, fc, 8 * t)
+            if t == lo - 1:
+                new = [jnp.where(has_low, x, 0.0) for x in new]
+            if t == hi:
+                new = [jnp.where(has_high, x, 0.0) for x in new]
+            at = pl.ds(8 * t, 8)
+            for i, x in enumerate(new):
+                dst[i * cols : (i + 1) * cols, at] = x
+            if not last:
+                products(new, ref, at, new_tmp)
+
+    for j in (1, 2, 3):
+        step(j, 2)
 
     def pair(_, carry):
-        step(b, a, lo - 1, lo + 5)
-        step(a, b, lo - 1, lo + 5)
+        for j in (4, 5, 6, 7):
+            step(j, 1)
         return carry
 
-    lax.fori_loop(0, 4, pair, 0)
-    step(b, a, lo, lo + 4)
+    lax.fori_loop(0, 2, pair, 0)
+    step(STEPS, 0, last=True)
 
 
 def kernel(
     tms, strips, total_rows,
     inc_hbm, depth_hbm, wind_hbm, spread_hbm, decay_hbm, out_ref,
-    raw, fa, fb, ref, tmp, fc, spread, decay,
-    halo_out, halo_in, pre_out, pre_in, tan_out, tan_in, scan_b, w_own, w_in, wl_in, wh_in, wk_in, wk,
-    load_sem, halo_send, halo_recv, pre_send, pre_recv, tan_send, tan_recv,
+    raw, fa, fb, ref, tmp_a, tmp_b, fc, spread, decay,
+    halo_out, halo_in, pre_out, pre_in, inc_out, inc_in, mate, tan_out, tan_in, scan_b, w_own, w_in, wl_in, wh_in, wk_in, wk,
+    load_sem, halo_send, halo_recv, pre_send, pre_recv, inc_send, inc_recv, mate_send, mate_recv, tan_send, tan_recv,
     w_send, w_recv, wh_send, wl_recv, wh_recv, wk_send, wk_recv,
 ):
     nine = fa.shape[0]
     cols = nine // 3
     rows = spread.shape[1]
     per = rows // tms
+    flat = per * nine
+    bufs = ((fa, tmp_a), (fb, tmp_b))
     halo = STEPS
     edge = halo // per
     tm = lax.axis_index("tm")
     strip = lax.axis_index("strip")
     has_low, has_high = strip > 0, strip < strips - 1
+    even, odd = lax.rem(tm, 2) == 0, lax.rem(tm, 2) == 1
     to_low, to_high = jnp.logical_and(has_low, tm < edge), jnp.logical_and(has_high, tm >= tms - edge)
+
+    def partner(dy, dx, dc):
+        y, x, c = lax.div(tm, 4), lax.rem(lax.div(tm, 2), 2), lax.rem(tm, 2)
+        return 4 * lax.rem(y + dy, tms // 4) + 2 * (1 - x if dx else x) + (1 - c if dc else c)
+
+    def others_by(order):
+        return [partner(*way) for way in order if way != (0, 0, 0)]
 
     barrier = pltpu.get_barrier_semaphore()
 
@@ -217,21 +239,26 @@
         device_id=(tm, strip + 1), device_id_type=MESH,
     )
 
-    @pl.when(has_low)
+    across_above = lax.rem(strip, 2) == 0
+
+    @pl.when(jnp.logical_and(has_low, across_above))
     def _():
         to_below.start()
 
     @pl.when(has_high)
     def _():
         to_above.start()
+
+    @pl.when(jnp.logical_and(has_low, jnp.logical_not(across_above)))
+    def _():
+        to_below.start()
 
     def wait_for(slabs, sem):
         pltpu.make_async_copy(slabs, slabs, sem).wait()
 
     def spread_out(out, into, send, recv):
         copies = []
-        for d in range(1, tms):
-            to = lax.rem(tm + d, tms)
+        for to in others_by(ORDER):
             copies.append(pltpu.make_async_remote_copy(
                 out.at[to], into.at[tm], send, recv,
                 device_id=(to, strip), device_id_type=MESH,
@@ -247,9 +274,22 @@
     for i in range(nine):
         for j in range(tms):
             here = slice(per * j, per * (j + 1))
-            for n, part in enumerate((fa[i, TOP + per * j : TOP + per * (j + 1)], spread[i, here], decay[i, here])):
-                at = per * (n * nine + i)
-                pre_out[j, at : at + per] = part
+            inc_out[j, per * i : per * (i + 1)] = fa[i, TOP + per * j : TOP + per * (j + 1)]
+            pre_out[j, per * i : per * (i + 1)] = spread[i, here]
+            pre_out[j, flat + per * i : flat + per * (i + 1)] = decay[i, here]
+    to_mate = pltpu.make_async_remote_copy(
+        inc_out, mate, mate_send, mate_recv, device_id=(jnp.maximum(tm - 1, 0), strip), device_id_type=MESH
+    )
+
+    @pl.when(odd)
+    def _():
+        to_mate.start()
+        mate[...] = jnp.zeros_like(mate)
+
+    @pl.when(even)
+    def _():
+        spread_out(inc_out, inc_in, inc_send, inc_recv)
+
     spread_out(pre_out, pre_in, pre_send, pre_recv)
 
     @pl.when(has_low)
@@ -266,68 +306,75 @@
             for n, buf in ((0, fa), (nine, ref)):
                 buf[i, TOP + rows : TOP + rows + halo] = halo_in[1, (n + i) * halo : (n + i + 1) * halo]
 
-    run_steps(
-        lambda a, b, first, stop: tangent_step(a, b, ref, tmp, fc, first, stop, has_low, has_high), fa, fb
-    )
+    run_steps(tangent_tile, tangent_products, bufs, ref, fc, rows, has_low, has_high)
+    @pl.when(even)
+    def _():
+        to_mate.wait_recv()
+
     for i in range(nine):
         for j in range(tms):
-            tan_out[j, per * i : per * (i + 1)] = fa[i, TOP + per * j : TOP + per * (j + 1)]
+            at = slice(per * i, per * (i + 1))
+            tan_out[j, at] = mate[j, at] - fa[i, TOP + per * j : TOP + per * (j + 1)]
 
     spread_out(tan_out, tan_in, tan_send, tan_recv)
 
     others = pl.ds(0, tms - 1)
     wait_for(pre_in.at[others], pre_recv)
+
+    @pl.when(even)
+    def _():
+        wait_for(inc_in.at[pl.ds(0, tms // 2 - 1)], inc_recv)
+
+    @pl.when(odd)
+    def _():
+        wait_for(inc_in.at[pl.ds(0, tms // 2)], inc_recv)
+
     wait_for(tan_in.at[others], tan_recv)
-    flat = per * nine
     built = None
     for k in range(tms):
-        residual = pre_in[k, 0:flat]
-        if k:
-            residual = residual - tan_in[k - 1]
-        scaled = pre_in[k, flat : 2 * flat] * residual
-        built = scaled if k == 0 else pre_in[k, 2 * flat :] * built + scaled
+        residual = inc_in[k] if k == 0 else tan_in[k - 1] if k % 2 else inc_in[k] + tan_in[k - 1]
+        scaled = pre_in[k, 0:flat] * residual
+        built = scaled if k == 0 else pre_in[k, flat:] * built + scaled
         scan_b[k] = built
     w_own[tms] = jnp.zeros((flat, LANES), jnp.float32)
     smoothed = None
     for k in reversed(range(tms)):
-        smoothed = scan_b[k] if smoothed is None else scan_b[k] + pre_in[k + 1, 2 * flat :] * smoothed
-        w_own[k] = pre_in[k, flat : 2 * flat] * smoothed
-
-    w_copies, low_copies, high_copies, wk_copies = [], [], [], []
-    for d in range(tms):
-        to = lax.rem(tm + d, tms)
-        low_copies.append(pltpu.make_async_remote_copy(
+        smoothed = scan_b[k] if smoothed is None else scan_b[k] + pre_in[k + 1, flat:] * smoothed
+        w_own[k] = pre_in[k, 0:flat] * smoothed
+
+    def to_low_halo(to):
+        return pltpu.make_async_remote_copy(
             w_own.at[to + 1], wh_in.at[lax.rem(tm, edge)], wh_send, wh_recv,
             device_id=(to, strip - 1), device_id_type=MESH,
-        ))
-        high_copies.append(pltpu.make_async_remote_copy(
-            w_own.at[to + 1], wl_in.at[lax.rem(tm + edge - (tms - edge) % edge, edge)], wh_send, wl_recv,
+        )
+
+    def to_high_halo(to):
+        at = lax.rem(tm + edge - (tms - edge) % edge, edge)
+        return pltpu.make_async_remote_copy(
+            w_own.at[to + 1], wl_in.at[at], wh_send, wl_recv,
             device_id=(to, strip + 1), device_id_type=MESH,
-        ))
-        if d:
-            w_copies.append(pltpu.make_async_remote_copy(
-                w_own.at[to + 1], w_in.at[tm], w_send, w_recv,
-                device_id=(to, strip), device_id_type=MESH,
-            ))
-            wk_copies.append(pltpu.make_async_remote_copy(
-                w_own.at[to], wk_in.at[tm], wk_send, wk_recv,
-                device_id=(to, strip), device_id_type=MESH,
-            ))
-
-    @pl.when(to_low)
-    def _():
-        for copy in low_copies:
-            copy.start()
-
-    @pl.when(to_high)
-    def _():
-        for copy in high_copies:
-            copy.start()
-
-    for copy in w_copies:
-        copy.start()
-    for copy in wk_copies:
-        copy.start()
+        )
+
+    def to_same(to, shift, into, send, recv):
+        return pltpu.make_async_remote_copy(
+            w_own.at[to + shift], into.at[tm], send, recv, device_id=(to, strip), device_id_type=MESH
+        )
+
+    for ways, halo_ways in RETURN:
+        @pl.when(to_low)
+        def _():
+            for way in halo_ways:
+                to_low_halo(partner(*way)).start()
+
+        @pl.when(to_high)
+        def _():
+            for way in halo_ways:
+                to_high_halo(partner(*way)).start()
+
+        for to in others_by(ways):
+            to_same(to, 1, w_in, w_send, w_recv).start()
+    for to in others_by(ORDER):
+        to_same(to, 0, wk_in, wk_send, wk_recv).start()
     w_in[tm] = w_own[tm + 1]
     wk_in[tm] = w_own[tm]
 
@@ -360,9 +407,7 @@
         for q in range(edge):
             unpack(wh_in.at[q], TOP + rows + per * q)
 
-    run_steps(
-        lambda a, b, first, stop: adjoint_step(a, b, ref, tmp, fc, first, stop, has_low, has_high), fa, fb
-    )
+    run_steps(adjoint_tile, adjoint_products, bufs, ref, fc, rows, has_low, has_high)
     wait_for(wk_in.at[others], wk_recv)
     for j in range(tms):
         for i in range(nine):
@@ -390,6 +435,14 @@
     @pl.when(jnp.logical_or(to_low, to_high))
     def _():
         wait_for(w_own.at[pl.ds(0, tms)], wh_send)
+
+    @pl.when(even)
+    def _():
+        wait_for(inc_out.at[others], inc_send)
+
+    @pl.when(odd)
+    def _():
+        to_mate.wait_send()
 
     for slabs, sem in ((pre_out, pre_send), (tan_out, tan_send), (w_own, w_send), (w_own, wk_send)):
         wait_for(slabs.at[others], sem)
@@ -415,15 +468,16 @@
         scratch_shapes=[
             vmem(4, planes, rows, width),
             vmem(nine, height, LANES), vmem(nine, height, LANES), vmem(nine, height, LANES),
-            vmem(2 * cols, height, LANES), vmem(height, LANES),
+            vmem(2 * cols, height, LANES), vmem(2 * cols, height, LANES), vmem(height, LANES),
             vmem(nine, rows, LANES), vmem(nine, rows, LANES),
             vmem(2, 2 * nine * STEPS, LANES), vmem(2, 2 * nine * STEPS, LANES),
-            vmem(tms, 3 * flat, LANES), vmem(tms, 3 * flat, LANES),
+            vmem(tms, 2 * flat, LANES), vmem(tms, 2 * flat, LANES),
+            vmem(tms, flat, LANES), vmem(tms, flat, LANES), vmem(tms, flat, LANES),
             vmem(tms, flat, LANES), vmem(tms, flat, LANES),
             vmem(tms, flat, LANES), vmem(tms + 1, flat, LANES), vmem(tms, flat, LANES),
             vmem(edge, flat, LANES), vmem(edge, flat, LANES), vmem(tms, flat, LANES),
             vmem(nine, rows, LANES),
-            dma((5,)), dma((2,)), dma((2,)), *[dma] * 11,
+            dma((5,)), dma((2,)), dma((2,)), *[dma] * 15,
         ],
         compiler_params=pltpu.CompilerParams(
             collective_id=0, has_side_effects=True, vmem_limit_bytes=24 * 2**20

time: 30 us -> 29.8 us (level)
  no operation moved by 1% of the time
where the time goes in v3:
time: 29.8 us; the launch traced here: 29.7 us
  Pallas kernels  29 us (97%)
  local copies, waits for them, and re-layouts  0.66 us (2%)
    pallas_call x1, Pallas kernels, body(): pl.pallas_call(functools.partial(kernel, tms, strips, strips * rows), out...  29 us
    unnamed x1, local copies, waits for them, and re-layouts  0.66 us

profile of v3, /device:TPU:385, one launch (start us, length us, event | category | flops | bytes accessed | tf_op | source)
XLA Modules:
  0.0 29.7 jit_solution(5916277564318274194)
XLA Ops:
  0.0 29.0 %shard_map.55 = f32[1,3,32,384]{3,2,1,0:T(8,128)S(1)} custom-call(f32[1,3,32,384]{3,2,1,0:T(8,128)} %inc_hbm.1, f32[1,1,32,384]{3,2,1,0:T(8,128)} %depth_hbm.1, f32[1,2,32,384]{3,2,1,0:T(8,128)} %wind_hbm.1, f32[1,3,32,384]{3,2,1,0:T(8,128)} %spread_hbm.1, f32[1,3,32,384]{3,2,1,0:T(8,128)} %decay_hbm.1), custom_call_target="tpu_custom_call" | custom-call | tf_op jit(solution)/shard_map/pallas_call | solution.py:463
  29.0 0.7 %copy.7 = f32[1,3,32,384]{3,2,1,0:T(8,128)} copy(f32[1,3,32,384]{3,2,1,0:T(8,128)S(1)} %shard_map.55) | data formatting | bytes 294912

commit v4 on v3

--- a/solution.py
+++ b/solution.py
@@ -96,11 +96,12 @@
     return new_p, new_q, new_s
 
 
-def run_steps(tile, products, bufs, ref, fc, rows, has_low, has_high):
+def run_steps(tile, products, bufs, ref, fc, rows, has_low, has_high, spreads):
     lo, hi = TOP // 8, (TOP + rows) // 8
     cols = ref.shape[0] // 3
 
-    for t in range(lo - 2, hi + 2):
+    reach = 1 if spreads else 2
+    for t in range(lo - reach, hi + reach):
         at = pl.ds(8 * t, 8)
         products([bufs[0][0][i * cols : (i + 1) * cols, at] for i in range(3)], ref, at, bufs[0][1])
 
@@ -118,24 +119,31 @@
             if not last:
                 products(new, ref, at, new_tmp)
 
-    for j in (1, 2, 3):
-        step(j, 2)
-
-    def pair(_, carry):
-        for j in (4, 5, 6, 7):
-            step(j, 1)
-        return carry
-
-    lax.fori_loop(0, 2, pair, 0)
-    step(STEPS, 0, last=True)
+    def four(first):
+        def turn(_, carry):
+            for j in range(first, first + 4):
+                step(j, 1)
+            return carry
+
+        lax.fori_loop(0, 2, turn, 0)
+
+    if spreads:
+        four(1)
+        for j in range(9, STEPS + 1):
+            step(j, 2, last=j == STEPS)
+    else:
+        for j in (1, 2, 3):
+            step(j, 2)
+        four(4)
+        step(STEPS, 0, last=True)
 
 
 def kernel(
     tms, strips, total_rows,
     inc_hbm, depth_hbm, wind_hbm, spread_hbm, decay_hbm, out_ref,
     raw, fa, fb, ref, tmp_a, tmp_b, fc, spread, decay,
-    halo_out, halo_in, pre_out, pre_in, inc_out, inc_in, mate, tan_out, tan_in, scan_b, w_own, w_in, wl_in, wh_in, wk_in, wk,
-    load_sem, halo_send, halo_recv, pre_send, pre_recv, inc_send, inc_recv, mate_send, mate_recv, tan_send, tan_recv,
+    halo_out, halo_in, pre_out, pre_in, inc_out, inc_in, mate, tan_out, tan_in, beside_out, beside_in, scan_b, w_own, w_in, wl_in, wh_in, wk_in, wk,
+    load_sem, halo_send, halo_recv, pre_send, pre_recv, inc_send, inc_recv, mate_send, mate_recv, tan_send, tan_recv, beside_send, beside_recv,
     w_send, w_recv, wh_send, wl_recv, wh_recv, wk_send, wk_recv,
 ):
     nine = fa.shape[0]
@@ -193,32 +201,28 @@
                 new = take_lanes(choose(marks, parts, j), into[j])
                 buf[p * cols + j, pl.ds(offset + 8 * t, 8)] = new * scale if scale else new
 
-    @pl.when(jnp.logical_not(has_low))
-    def _():
-        for buf in (fa, ref):
-            buf[:, TOP - 16 : TOP] = jnp.zeros((nine, 16, LANES), jnp.float32)
-
-    @pl.when(jnp.logical_not(has_high))
-    def _():
-        for buf in (fa, ref):
-            buf[:, TOP + rows : TOP + rows + 16] = jnp.zeros((nine, 16, LANES), jnp.float32)
+    for buf in (fa, fb, ref, tmp_a, tmp_b):
+        nothing = jnp.zeros((buf.shape[0], 16, LANES), jnp.float32)
+        buf[:, TOP - 16 : TOP] = nothing
+        buf[:, TOP + rows : TOP + rows + 16] = nothing
+
+    @pl.when(jnp.logical_not(jnp.logical_or(to_low, to_high)))
+    def _():
+        beside_in[...] = jnp.zeros_like(beside_in)
 
     row = lax.broadcasted_iota(jnp.int32, fc.shape, 0) + (strip * rows - TOP)
     fc[...] = DT * (0.2 + 0.4 * row.astype(jnp.float32) / total_rows)
 
-    loads[0].wait()
-    for p in range(3):
-        regroup(0, p, fa, TOP, HALF if p == 0 else None)
     loads[1].wait()
     loads[2].wait()
     for p in range(3):
         regroup(1, p, ref, TOP, HALF * HALF if p == 0 else HALF)
-
+    rest = halo_out.shape[1] - nine * halo
+    halo_out[:, nine * halo :] = jnp.zeros((2, rest, LANES), jnp.float32)
     for i in range(nine):
-        for n, buf in ((0, fa), (nine, ref)):
-            at = (n + i) * halo
-            halo_out[0, at : at + halo] = buf[i, TOP : TOP + halo]
-            halo_out[1, at : at + halo] = buf[i, TOP + rows - halo : TOP + rows]
+        at = i * halo
+        halo_out[0, at : at + halo] = ref[i, TOP : TOP + halo]
+        halo_out[1, at : at + halo] = ref[i, TOP + rows - halo : TOP + rows]
 
     inside = jnp.logical_and(has_low, has_high)
 
@@ -267,6 +271,9 @@
             copy.start()
         into[tm] = out[tm]
 
+    loads[0].wait()
+    for p in range(3):
+        regroup(0, p, fa, TOP, HALF if p == 0 else None)
     for n, buf in ((2, spread), (3, decay)):
         loads[n + 1].wait()
         for p in range(3):
@@ -296,17 +303,37 @@
     def _():
         to_above.wait_recv()
         for i in range(nine):
-            for n, buf in ((0, fa), (nine, ref)):
-                buf[i, TOP - halo : TOP] = halo_in[0, (n + i) * halo : (n + i + 1) * halo]
+            ref[i, TOP - halo : TOP] = halo_in[0, i * halo : (i + 1) * halo]
 
     @pl.when(has_high)
     def _():
         to_below.wait_recv()
         for i in range(nine):
-            for n, buf in ((0, fa), (nine, ref)):
-                buf[i, TOP + rows : TOP + rows + halo] = halo_in[1, (n + i) * halo : (n + i + 1) * halo]
-
-    run_steps(tangent_tile, tangent_products, bufs, ref, fc, rows, has_low, has_high)
+            ref[i, TOP + rows : TOP + rows + halo] = halo_in[1, i * halo : (i + 1) * halo]
+
+    run_steps(tangent_tile, tangent_products, bufs, ref, fc, rows, has_low, has_high, True)
+    for i in range(nine):
+        for q in range(edge):
+            at = slice(per * i, per * (i + 1))
+            beside_out[tms - edge + q, at] = fa[i, TOP - halo + per * q : TOP - halo + per * (q + 1)]
+            beside_out[q, at] = fa[i, TOP + rows + per * q : TOP + rows + per * (q + 1)]
+
+    def to_beside(to, beside):
+        return pltpu.make_async_remote_copy(
+            beside_out.at[to], beside_in.at[tm], beside_send, beside_recv,
+            device_id=(to, beside), device_id_type=MESH,
+        )
+
+    @pl.when(has_low)
+    def _():
+        for n in range(edge):
+            to_beside(tms - edge + lax.rem(tm + n, edge), strip - 1).start()
+
+    @pl.when(has_high)
+    def _():
+        for n in range(edge):
+            to_beside(lax.rem(tm + n, edge), strip + 1).start()
+
     @pl.when(even)
     def _():
         to_mate.wait_recv()
@@ -330,9 +357,18 @@
         wait_for(inc_in.at[pl.ds(0, tms // 2)], inc_recv)
 
     wait_for(tan_in.at[others], tan_recv)
+    @pl.when(jnp.logical_or(to_low, to_high))
+    def _():
+        wait_for(beside_in, beside_recv)
+
     built = None
     for k in range(tms):
-        residual = inc_in[k] if k == 0 else tan_in[k - 1] if k % 2 else inc_in[k] + tan_in[k - 1]
+        if k == 0:
+            residual = inc_in[k]
+        else:
+            residual = tan_in[k - 1] - beside_in[k - 1]
+            if k % 2 == 0:
+                residual = inc_in[k] + residual
         scaled = pre_in[k, 0:flat] * residual
         built = scaled if k == 0 else pre_in[k, flat:] * built + scaled
         scan_b[k] = built
@@ -407,7 +443,7 @@
         for q in range(edge):
             unpack(wh_in.at[q], TOP + rows + per * q)
 
-    run_steps(adjoint_tile, adjoint_products, bufs, ref, fc, rows, has_low, has_high)
+    run_steps(adjoint_tile, adjoint_products, bufs, ref, fc, rows, has_low, has_high, False)
     wait_for(wk_in.at[others], wk_recv)
     for j in range(tms):
         for i in range(nine):
@@ -426,6 +462,14 @@
 
     @pl.when(has_low)
     def _():
+        wait_for(beside_out.at[pl.ds(0, edge)], beside_send)
+
+    @pl.when(has_high)
+    def _():
+        wait_for(beside_out.at[pl.ds(0, edge)], beside_send)
+
+    @pl.when(has_low)
+    def _():
         to_below.wait_send()
 
     @pl.when(has_high)
@@ -456,6 +500,7 @@
     flat = per * nine
     edge = STEPS // per
     height = rows + 2 * TOP
+    edge_rows = -(-nine * STEPS // 8) * 8
     dma = pltpu.SemaphoreType.DMA
     f32 = jnp.float32
     vmem = lambda *shape: pltpu.VMEM(shape, f32)
@@ -470,14 +515,14 @@
             vmem(nine, height, LANES), vmem(nine, height, LANES), vmem(nine, height, LANES),
             vmem(2 * cols, height, LANES), vmem(2 * cols, height, LANES), vmem(height, LANES),
             vmem(nine, rows, LANES), vmem(nine, rows, LANES),
-            vmem(2, 2 * nine * STEPS, LANES), vmem(2, 2 * nine * STEPS, LANES),
+            vmem(2, edge_rows, LANES), vmem(2, edge_rows, LANES),
             vmem(tms, 2 * flat, LANES), vmem(tms, 2 * flat, LANES),
             vmem(tms, flat, LANES), vmem(tms, flat, LANES), vmem(tms, flat, LANES),
-            vmem(tms, flat, LANES), vmem(tms, flat, LANES),
+            vmem(tms, flat, LANES), vmem(tms, flat, LANES), vmem(tms, flat, LANES), vmem(tms, flat, LANES),
             vmem(tms, flat, LANES), vmem(tms + 1, flat, LANES), vmem(tms, flat, LANES),
             vmem(edge, flat, LANES), vmem(edge, flat, LANES), vmem(tms, flat, LANES),
             vmem(nine, rows, LANES),
-            dma((5,)), dma((2,)), dma((2,)), *[dma] * 15,
+            dma((5,)), dma((2,)), dma((2,)), *[dma] * 17,
         ],
         compiler_params=pltpu.CompilerParams(
             collective_id=0, has_side_effects=True, vmem_limit_bytes=24 * 2**20

time: 29.8 us -> 29.5 us (0.990)
  Pallas kernels: 29 us -> 28.7 us
where the time goes in v4:
time: 29.5 us; the launch traced here: 29.4 us
  Pallas kernels  28.7 us (97%)
  local copies, waits for them, and re-layouts  0.66 us (2%)
    pallas_call x1, Pallas kernels, body(): pl.pallas_call(functools.partial(kernel, tms, strips, strips * rows), out...  28.7 us
    unnamed x1, local copies, waits for them, and re-layouts  0.66 us

profile of v4, /device:TPU:385, one launch (start us, length us, event | category | flops | bytes accessed | tf_op | source)
XLA Modules:
  0.0 29.4 jit_solution(2483592248642303840)
XLA Ops:
  0.0 28.7 %shard_map.55 = f32[1,3,32,384]{3,2,1,0:T(8,128)S(1)} custom-call(f32[1,3,32,384]{3,2,1,0:T(8,128)} %inc_hbm.1, f32[1,1,32,384]{3,2,1,0:T(8,128)} %depth_hbm.1, f32[1,2,32,384]{3,2,1,0:T(8,128)} %wind_hbm.1, f32[1,3,32,384]{3,2,1,0:T(8,128)} %spread_hbm.1, f32[1,3,32,384]{3,2,1,0:T(8,128)} %decay_hbm.1), custom_call_target="tpu_custom_call" | custom-call | tf_op jit(solution)/shard_map/pallas_call | solution.py:508
  28.7 0.7 %copy.7 = f32[1,3,32,384]{3,2,1,0:T(8,128)} copy(f32[1,3,32,384]{3,2,1,0:T(8,128)S(1)} %shard_map.55) | data formatting | bytes 294912

commit v5 on v4

--- a/solution.py
+++ b/solution.py
@@ -326,13 +326,15 @@
 
     @pl.when(has_low)
     def _():
-        for n in range(edge):
-            to_beside(tms - edge + lax.rem(tm + n, edge), strip - 1).start()
-
-    @pl.when(has_high)
-    def _():
-        for n in range(edge):
-            to_beside(lax.rem(tm + n, edge), strip + 1).start()
+        @pl.loop(tms - edge, tms)
+        def _(to):
+            to_beside(to, strip - 1).start()
+
+    @pl.when(has_high)
+    def _():
+        @pl.loop(0, edge)
+        def _(to):
+            to_beside(to, strip + 1).start()
 
     @pl.when(even)
     def _():

time: 29.5 us -> 29.4 us (level)
  no operation moved by 1% of the time
where the time goes in v5:
time: 29.4 us; the launch traced here: 29.3 us
  Pallas kernels  28.6 us (97%)
  local copies, waits for them, and re-layouts  0.66 us (2%)
    pallas_call x1, Pallas kernels, body(): pl.pallas_call(functools.partial(kernel, tms, strips, strips * rows), out...  28.6 us
    unnamed x1, local copies, waits for them, and re-layouts  0.66 us

profile of v5, /device:TPU:385, one launch (start us, length us, event | category | flops | bytes accessed | tf_op | source)
XLA Modules:
  0.0 29.3 jit_solution(9925950153196802856)
XLA Ops:
  0.0 28.6 %shard_map.55 = f32[1,3,32,384]{3,2,1,0:T(8,128)S(1)} custom-call(f32[1,3,32,384]{3,2,1,0:T(8,128)} %inc_hbm.1, f32[1,1,32,384]{3,2,1,0:T(8,128)} %depth_hbm.1, f32[1,2,32,384]{3,2,1,0:T(8,128)} %wind_hbm.1, f32[1,3,32,384]{3,2,1,0:T(8,128)} %spread_hbm.1, f32[1,3,32,384]{3,2,1,0:T(8,128)} %decay_hbm.1), custom_call_target="tpu_custom_call" | custom-call | tf_op jit(solution)/shard_map/pallas_call | solution.py:510
  28.6 0.7 %copy.7 = f32[1,3,32,384]{3,2,1,0:T(8,128)} copy(f32[1,3,32,384]{3,2,1,0:T(8,128)S(1)} %shard_map.55) | data formatting | bytes 294912
